TPU v7x, 128 devices: a whole 4x4x4 slice. The times are simulated.
128 devices in a mesh: row: 8 (over x, y_hi), col: 16 (over y_lo, z, core).
Axes of the slice: x: 4, y: 4 (y_hi: 2, y_lo: 2; y = y_hi * 2 + y_lo), z: 4, core: 2. Of those that a mesh axis runs over, the one named last changes fastest.
Arguments:
- amplitude: float32 [800, 20480], P('row', 'col'), may hold values from -6 to 6
- ladder_coupling: float32 [20480, 20480], P('row', 'col'), may hold values from -0.0390625 to 0.0390625
- crossed_coupling: float32 [8, 1280, 1280], P('row'), may hold values from -0.15625 to 0.15625
- channel_slot: int32 [8], replicated, may hold values from 0 to 7, each once
- channel_of: int32 [16, 1024, 1], P('col', 'row'), may hold values from 0 to 7; in each aligned block of 128 rows (0 to 127, 128 to 255, ..., all dimensions but the last counted through in order) at most 40 rows name the same one
- source_row: int32 [16, 1024], P('col', 'row'), may hold values from 0 to 799
- target_row: int32 [16, 1024], P('col', 'row'), may hold values from 0 to 1599
- recoupling: float32 [16, 1024], P('col', 'row'), may hold values from -1 to 1
- driving: float32 [800, 20480], P('col', 'row'), may hold values from -6 to 6
- denominator: float32 [800, 20480], P('col', 'row'), may hold values from 1 to 10
Outputs:
- updated: float32 [800, 20480], P('col', 'row')
Inputs may be any that keep to these rules, and one draw needn't show every extreme that they name: Among the 128 segments of one device (aligned blocks of channel_of's rows), no channel is named more than 40 times; some channel is named exactly 40 times in some device's segments. `channel_slot`: each slot once.
All inputs are finite; a program needn't handle non-finite values.
Results may differ from a plain program's by a relative error of at most 0.0003.
Values sent between devices are 32-bit elements; how exact they have to be, the bound alone decides.
A program may use at most 128 MiB of HBM per device.

v0:
```python
import jax
import jax.numpy as jnp
from jax import lax
from jax.sharding import PartitionSpec as P

CAP = 40


def on_device(
    amplitude,
    ladder_coupling,
    crossed_coupling,
    channel_slot,
    channel_of,
    source_row,
    target_row,
    recoupling,
    driving,
    denominator,
):
    highest = lax.Precision.HIGHEST
    gathered = lax.all_gather(amplitude, "row", axis=0, tiled=True)
    hole_pairs = gathered.shape[0]
    segment_width = crossed_coupling.shape[1]
    row_width = ladder_coupling.shape[0]
    groups = lax.axis_size("row")
    capacity = CAP
    picked = gathered[source_row[0]] * recoupling[0][:, None]
    owners = channel_slot[channel_of[0, :, 0]]
    onehot = (owners[:, None] == jnp.arange(groups, dtype=jnp.int32)[None, :]).astype(jnp.int32)
    before = jnp.cumsum(onehot, axis=0) - onehot
    placed = jnp.sum(before * onehot, axis=1)
    target = owners * capacity + placed
    buffer = jnp.zeros((groups * capacity, segment_width), jnp.float32).at[target].set(picked)
    buffer = buffer.reshape(groups, capacity, segment_width)
    mixture = jnp.einsum(
        "plf,fm->plm",
        lax.all_to_all(buffer, "row", split_axis=0, concat_axis=0, tiled=True),
        crossed_coupling[0],
        precision=highest,
        preferred_element_type=jnp.float32,
    )
    returned = lax.all_to_all(mixture, "row", split_axis=0, concat_axis=0, tiled=True)
    back_rows = returned.reshape(groups * capacity, segment_width)[target]
    spread = (
        jnp.zeros((hole_pairs * (row_width // segment_width), segment_width), jnp.float32)
        .at[target_row[0]]
        .add(back_rows)
    )
    particle_hole = spread.reshape(hole_pairs, row_width)
    partial_value = (
        lax.dot_general(
            gathered,
            ladder_coupling,
            (((1,), (1,)), ((), ())),
            precision=highest,
            preferred_element_type=jnp.float32,
        )
        + particle_hole
    )
    summed = lax.psum_scatter(partial_value, "col", scatter_dimension=0, tiled=True)
    return (driving + summed) / denominator


def solution(mesh):
    in_specs = (
        P("row", "col"),
        P("row", "col"),
        P("row", None, None),
        P(),
        P("col", "row", None),
        P("col", "row"),
        P("col", "row"),
        P("col", "row"),
        P("col", "row"),
        P("col", "row"),
    )
    out_specs = P("col", "row")
    return jax.shard_map(
        on_device, mesh=mesh, in_specs=in_specs, out_specs=out_specs, check_vma=False
    )
```

profile of v0, /device:TPU:1, one launch (start us, length us, event | category | flops | bytes accessed | tf_op | source)
XLA Modules:
  0.0 293.9 jit_solution(2602598759181581607)
XLA Ops:
  6.5 0.0 all-gather.3.cloned.1.call-start
  6.5 0.7 all-gather.3.cloned.1.call-update
  7.3 1.6 fusion.17
  8.9 5.7 %bitcast_select_fusion = s32[128]{0:T(128)S(1)} fusion(s32[1,128,1]{1,2,0:T(1,128)} %param.14, s32[]{:T(128)} %bitcast.6, s32[]{:T(128)} %bitcast.7, s32[]{:T(128)} %bitcast.8, s32[]{:T(128)} %bitcast.9, s32[]{:T(128)} %bitcast.10, s32[]{:T(128)} %bitcast.12, s32[]{:T(128)} %bitcast.11, s32[]{:T(128)} %bitcast.5), kind=kLoop, calls=%fused_computation.25 | loop fusion | flops 2176 | bytes 1056 | tf_op jit(solution)/shard_map/gather | solution.py:29
  14.5 0.1 fusion.11
  14.6 0.2 reduce_window_sum.11
  14.8 0.7 fusion.15
  15.5 0.2 select_reduce_fusion
  15.6 5.7 %fusion.14 = s32[128]{0:T(128)S(1)} fusion(s32[128]{0:T(128)S(1)} %select_reduce_fusion, s32[]{:T(128)} %bitcast.12, s32[]{:T(128)} %bitcast.11, s32[]{:T(128)} %bitcast.10, s32[]{:T(128)} %bitcast.9, s32[]{:T(128)} %bitcast.8, s32[]{:T(128)} %bitcast.7, s32[]{:T(128)} %bitcast.6, s32[]{:T(128)} %bitcast.5, s32[1,128,1]{1,2,0:T(1,128)} %param.14), kind=kLoop, calls=%fused_computation.34 | loop fusion | flops 2816 | bytes 1568 | tf_op jit(solution)/shard_map/select_n | solution.py:34
  21.3 63.2 %all-gather.3.cloned.1.call-done = f32[8,100,1280]{2,1,0:T(8,128)} async-done(((f32[1,100,1280]{2,1,0:T(8,128)}), f32[8,100,1280]{2,1,0:T(8,128)}) %all-gather.3.cloned.1.call-update) | async-done | bytes 4096016 | tf_op jit(solution)/shard_map/all_gather | solution.py:22
  84.6 3.7 %reshape.193 = f32[800,1280]{1,0:T(8,128)} reshape(f32[8,100,1280]{2,1,0:T(8,128)} %all-gather.3.cloned.1.call-done) | data formatting | bytes 8192000
  88.3 0.0 copy-done.4
  88.3 3.3 %scatter_custom_fusion = f32[320,1280]{1,0:T(8,128)S(1)} fusion(s32[128]{0:T(128)S(1)} %fusion.14, f32[]{:T(128)} %constant.7.clone.1, f32[128]{0:T(128)S(1)} %bitcast.51, f32[800,1280]{1,0:T(8,128)} %reshape.193, s32[1024]{0:T(1024)S(1)} %pad_clamp_fusion.1), kind=kCustom, calls=%fused_computation.9 | custom fusion | flops 163840 | bytes 5739012 | tf_op jit(solution)/shard_map/scatter | solution.py:34
  91.7 24.3 %all_to_all.10 = f32[8,40,1280]{2,1,0:T(8,128)S(1)} all-to-all(f32[8,40,1280]{2,1,0:T(8,128)S(1)} %bitcast.48), channel_id=1, replica_groups=mesh['row'=8,'col'=16] {'row'}, dimensions={0} | all-to-all | bytes 3276800 | tf_op jit(solution)/shard_map/all_to_all | solution.py:38
  115.9 10.9 %fusion.1 = f32[8,40,1280]{2,1,0:T(8,128)} fusion(f32[8,40,1280]{2,1,0:T(8,128)S(1)} %all_to_all.10, f32[1,1280,1280]{2,1,0:T(8,128)} %param.12), kind=kOutput, calls=%fused_computation.4 | convolution fusion | flops 6291456000 | bytes 9830400 | tf_op jit(solution)/shard_map/plf,fm->plm/dot_general | solution.py:36
  126.8 3.6 %all-to-all-start.1 = ((f32[8,40,1280]{2,1,0:T(8,128)}), f32[8,40,1280]{2,1,0:T(8,128)S(1)}, u32[]{:S(2)}, u32[]{:S(2)}) async-start(f32[8,40,1280]{2,1,0:T(8,128)} %fusion.1), calls=%async_computation.1 | async-start | bytes 3276800 | tf_op jit(solution)/shard_map/all_to_all | solution.py:43
  130.4 0.0 copy-done.5
  130.5 21.7 %all-to-all-done.1 = f32[8,40,1280]{2,1,0:T(8,128)S(1)} async-done(((f32[8,40,1280]{2,1,0:T(8,128)}), f32[8,40,1280]{2,1,0:T(8,128)S(1)}, u32[]{:S(2)}, u32[]{:S(2)}) %all-to-all-start.1) | async-done | bytes 1638432 | tf_op jit(solution)/shard_map/all_to_all | solution.py:43
  152.2 6.1 %scatter_custom_fusion.1 = f32[1600,1280]{1,0:T(8,128)} fusion(s32[128]{0:T(128)S(1)} %fusion.13, f32[]{:T(128)} %constant.7.clone.1, f32[320,1280]{1,0:T(8,128)S(1)} %bitcast.49, s32[1024]{0:T(1024)S(1)} %pad_clamp_fusion), kind=kCustom, calls=%fused_computation.7 | custom fusion | flops 163840 | bytes 8192004 | tf_op jit(solution)/shard_map/scatter-add | solution.py:48
  158.3 9.8 %reshape.123 = f32[800,2560]{1,0:T(8,128)} reshape(f32[1600,1280]{1,0:T(8,128)} %scatter_custom_fusion.1) | data formatting | bytes 16384000 | tf_op jit(solution)/shard_map/reshape | solution.py:50
  168.1 37.6 %convolution_add_fusion = f32[800,2560]{1,0:T(8,128)} fusion(f32[800,2560]{1,0:T(8,128)} %reshape.123, f32[800,1280]{1,0:T(8,128)} %reshape.193, f32[2560,1280]{1,0:T(8,128)} %param.11), kind=kOutput, calls=%fused_computation.6 | convolution fusion | flops 31459328000 | bytes 33587200 | tf_op jit(solution)/shard_map/dot_general | solution.py:52
  205.7 56.1 %fusion = f32[56,2560]{1,0:T(8,128)S(1)} fusion(f32[800,2560]{1,0:T(8,128)} %convolution_add_fusion), kind=kCustom, calls=%all-reduce-scatter | all-reduce-scatter fusion | flops 2293761 | bytes 8765952
  261.8 0.0 copy-start
  261.8 0.0 copy-start.1
  261.9 4.5 %collective-permute-start = (f32[56,2560]{1,0:T(8,128)S(1)}, f32[56,2560]{1,0:T(8,128)}, u32[]{:S(2)}, u32[]{:S(2)}) collective-permute-start(f32[56,2560]{1,0:T(8,128)S(1)} %fusion), channel_id=1, source_target_pairs={{0,1},{1,2},{2,3},{3,4},{4,5},{5,6},{6,7},{7,8},{8,9},{9,10},{10,1... | collective-permute-start | bytes 1720328
  266.4 3.2 %collective-permute-start.1 = (f32[34,2560]{1,0:T(8,128)S(1)}, f32[34,2560]{1,0:T(8,128)S(1)}, u32[]{:S(2)}, u32[]{:S(2)}) collective-permute-start(f32[34,2560]{1,0:T(8,128)S(1)} %slice.13), channel_id=1, source_target_pairs={{0,2},{1,3},{2,4},{3,5},{4,6},{5,7},{6,8},{7,9},{8,10},{9,11},{10,... | collective-permute-start | bytes 1044488
  269.6 0.6 dynamic-slice.4
  270.8 10.9 %collective-permute-done.1 = f32[34,2560]{1,0:T(8,128)S(1)} collective-permute-done((f32[34,2560]{1,0:T(8,128)S(1)}, f32[34,2560]{1,0:T(8,128)S(1)}, u32[]{:S(2)}, u32[]{:S(2)}) %collective-permute-start.1) | collective-permute-done | bytes 348192
  281.8 0.7 copy-done.2
  282.5 0.0 collective-permute-done
  282.5 3.5 %concatenate = f32[146,2560]{1,0:T(8,128)S(1)} concatenate(f32[34,2560]{1,0:T(8,128)} %copy-done.2, f32[56,2560]{1,0:T(8,128)} %collective-permute-done, f32[56,2560]{1,0:T(8,128)S(1)} %fusion), dimensions={0} | concatenate | bytes 2990080
  286.1 0.9 fusion.9
  (11 shorter events, 0.1 us)
Async XLA Ops:
  6.5 78.0 %all-gather.3.cloned.1.call-start = ((), (), s32[]{:S(2)}) async-start(), calls=%async_computation.2 | async-start | bytes 4792320 | tf_op jit(solution)/shard_map/all_gather | solution.py:22
  21.3 67.0 %copy-start.4 = (f32[1,128]{1,0:T(1,128)S(1)}, f32[1,128]{1,0:T(1,128)}, u32[]{:S(2)}) copy-start(f32[1,128]{1,0:T(1,128)} %param.17) | copy-start | bytes 1540
  115.9 14.5 %copy-start.5 = (s32[1,128]{1,0:T(1,128)S(1)}, s32[1,128]{1,0:T(1,128)}, u32[]{:S(2)}) copy-start(s32[1,128]{1,0:T(1,128)} %param.16) | copy-start | bytes 1540
  126.8 25.4 %all-to-all-start.1 = ((f32[8,40,1280]{2,1,0:T(8,128)}), f32[8,40,1280]{2,1,0:T(8,128)S(1)}, u32[]{:S(2)}, u32[]{:S(2)}) async-start(f32[8,40,1280]{2,1,0:T(8,128)} %fusion.1), calls=%async_computation.1 | async-start | bytes 3276800 | tf_op jit(solution)/shard_map/all_to_all | solution.py:43
  205.7 63.9 %copy-start.3 = (u32[128]{0:T(128)S(1)}, u32[128]{0:T(128)}, u32[]{:S(2)}) copy-start(u32[128]{0:T(128)} %constant.38) | copy-start | bytes 1540
  261.8 24.2 %copy-start = (f32[50,2560]{1,0:T(8,128)S(1)}, f32[50,2560]{1,0:T(8,128)}, u32[]{:S(2)}) copy-start(f32[50,2560]{1,0:T(8,128)} %param.19) | copy-start | bytes 1536004
  261.8 24.2 %copy-start.1 = (f32[50,2560]{1,0:T(8,128)S(1)}, f32[50,2560]{1,0:T(8,128)}, u32[]{:S(2)}) copy-start(f32[50,2560]{1,0:T(8,128)} %param.18) | copy-start | bytes 1536004
  261.9 20.7 %collective-permute-start = (f32[56,2560]{1,0:T(8,128)S(1)}, f32[56,2560]{1,0:T(8,128)}, u32[]{:S(2)}, u32[]{:S(2)}) collective-permute-start(f32[56,2560]{1,0:T(8,128)S(1)} %fusion), channel_id=1, source_target_pairs={{0,1},{1,2},{2,3},{3,4},{4,5},{5,6},{6,7},{7,8},{8,9},{9,10},{10,1... | collective-permute-start | bytes 1720328
  266.4 15.4 %collective-permute-start.1 = (f32[34,2560]{1,0:T(8,128)S(1)}, f32[34,2560]{1,0:T(8,128)S(1)}, u32[]{:S(2)}, u32[]{:S(2)}) collective-permute-start(f32[34,2560]{1,0:T(8,128)S(1)} %slice.13), channel_id=1, source_target_pairs={{0,2},{1,3},{2,4},{3,5},{4,6},{5,7},{6,8},{7,9},{8,10},{9,11},{10,... | collective-permute-start | bytes 1044488
  281.8 0.8 copy-start.2
Sparse Core Ops, SparseCore 0:
  9.7 74.8 all-gather.2
where the time goes:
time: 299 us; the launch traced here: 294 us
  waiting for transfers between devices  96.6 us (32%)
  blocking collectives  80.4 us (27%)
  matrix products  48.5 us (16%)
  other arithmetic  22.8 us (8%)
  local copies, waits for them, and re-layouts  20.1 us (7%)
  between operations  14.2 us (5%)
  starting transfers between devices  11.3 us (4%)
    all_gather x1, waiting for transfers between devices, on_device(): gathered = lax.all_gather(amplitude, 'row', axis=0, tiled=True)  63.2 us
    unnamed x1, blocking collectives  56.1 us
    dot_general x1, matrix products, on_device(): lax.dot_general(gathered, ladder_coupling, (((1,), (1,)), ((), ())), prec...  37.6 us
    all_to_all x1, blocking collectives, on_device(): lax.all_to_all(buffer, 'row', split_axis=0, concat_axis=0, tiled=True)  24.3 us
    all_to_all x1, waiting for transfers between devices, on_device(): lax.all_to_all(mixture, 'row', split_axis=0, concat_axis=0, tiled=True)  21.7 us
    unnamed x3, waiting for transfers between devices  11.7 us
    dot_general x1, matrix products, on_device(): jnp.einsum('plf,fm->plm', lax.all_to_all(buffer, 'row', split_axis=0, con...  10.9 us
    reshape x1, local copies, waits for them, and re-layouts, on_device(): particle_hole = spread.reshape(hole_pairs, row_width)  9.83 us
  transfers between devices with their start and end apart: 4, of which 3 were waited for; matrix products, arithmetic and copies ran while one was open for 5% of the time, Pallas kernels for 0%

commit v1 on v0

v1 whole, which is shorter than its diff:
```python
import jax
import jax.numpy as jnp
from jax import lax
from jax.experimental import pallas as pl
from jax.experimental.pallas import tpu as pltpu
from jax.sharding import PartitionSpec as P

CAP = 40
NROW = 8
PAD = 104
CHUNK = 256
MESH = pl.DeviceIdType.MESH
F32 = jnp.float32
BF16 = jnp.bfloat16
OFFSETS = [(dx, dy) for dx in (1, 3, 2, 0) for dy in (0, 1) if (dx, dy) != (0, 0)]


def split(value):
    high = value.astype(BF16)
    return high, (value - high.astype(F32)).astype(BF16)


def dot(a, b):
    return lax.dot_general(a, b, (((1,), (0,)), ((), ())), preferred_element_type=F32)


def dot_t(a, b):
    return lax.dot_general(a, b, (((1,), (1,)), ((), ())), preferred_element_type=F32)


def kernel(
    meta, tgt, amp, lad, xm, out,
    own, gath, ahi, alo, stage, chi, clo, xstage, xhi, xlo, mrecv, colb, colc, pacc, phi, plo, onehot,
    cross, back, sib, mine, crecv, zrecv, yrecv, esend, erecv,
    lsem, stsem, gs, gr, ms, mr, ts, tr, cs, cr, zs, zr, ys, yr, es, er,
):
    rows, width = amp.shape
    chunks = width // CHUNK
    half = width // 2
    r, c = lax.axis_index("row"), lax.axis_index("col")
    x, yh = r // 2, r % 2
    yl, z, core = c // 8, (c // 2) % 4, c % 2
    xp, xm1, x2 = (x + 1) % 4, (x + 3) % 4, (x + 2) % 4
    zp, zm, z2 = (z + 1) % 4, (z + 3) % 4, (z + 2) % 4

    def row_dev(i):
        dx, dy = OFFSETS[i]
        return ((x + dx) % 4) * 2 + (yh + dy) % 2

    def row_src(i):
        dx, dy = OFFSETS[i]
        return ((x + 4 - dx) % 4) * 2 + (yh + dy) % 2

    sibling = (r, yl * 8 + z * 2 + (1 - core))
    above = (r, yl * 8 + zp * 2 + core)
    below = (r, yl * 8 + zm * 2 + core)
    beside = (r, (1 - yl) * 8 + z * 2 + core)
    right, left, across = (xp * 2 + yh, c), (xm1 * 2 + yh, c), (x * 2 + 1 - yh, c)

    def remote(src, dst, send, recv, device):
        return pltpu.make_async_remote_copy(
            src_ref=src, dst_ref=dst, send_sem=send, recv_sem=recv, device_id=device, device_id_type=MESH
        )

    def load_ladder(p):
        return pltpu.make_async_copy(
            lad.at[pl.ds(pl.multiple_of(p * CHUNK, CHUNK), CHUNK), :], stage.at[p % 2], stsem.at[p % 2]
        )

    def load_cross(p):
        return pltpu.make_async_copy(
            xm.at[0, :, pl.ds(pl.multiple_of(p * CHUNK, CHUNK), CHUNK)], xstage.at[p % 2], stsem.at[2 + p % 2]
        )

    load_own = pltpu.make_async_copy(amp, own, lsem)
    load_own.start()
    load_ladder(0).start()
    load_cross(0).start()

    barrier = pltpu.get_barrier_semaphore()
    partners = [(row_dev(i), c) for i in range(7)] + [sibling, above, below, beside]
    for device in partners:
        pl.semaphore_signal(barrier, inc=1, device_id=device, device_id_type=MESH)
    load_own.wait()
    gath[r, 0:rows, :] = own[...]
    gath[r, rows:PAD, :] = jnp.zeros((PAD - rows, width), F32)
    pl.semaphore_wait(barrier, len(partners))

    def hop(i, shard, device, columns=None):
        ref = gath.at[shard] if columns is None else gath.at[shard, :, pl.ds(columns, half)]
        return remote(ref, ref, gs.at[i], gr.at[i], device)

    g1, g2, g3 = hop(0, r, right), hop(1, r, left), hop(2, r, across)
    g1.start()
    g2.start()
    g3.start()
    mcopies = []
    for i in range(7):
        copy = remote(meta.at[row_dev(i)], mrecv.at[r], ms.at[i], mr.at[i], (row_dev(i), c))
        copy.start()
        mcopies.append(copy)
    mrecv[r] = meta[r]

    @pl.loop(0, 2 * chunks)
    def _(p):
        load_ladder(p).wait()

        @pl.when(p + 1 < 2 * chunks)
        def _():
            load_ladder(p + 1).start()

        high, low = split(stage[p % 2])
        chi[p] = high
        clo[p] = low

    n_left, n_right, n_across = xm1 * 2 + yh, xp * 2 + yh, x * 2 + 1 - yh
    hop(0, n_left, right).wait_recv()
    g4 = hop(3, n_left, right, 0)
    g4.start()
    hop(1, n_right, left).wait_recv()
    g5 = hop(4, n_right, left, half)
    g5.start()
    hop(2, n_across, across).wait_recv()
    g6, g7 = hop(5, n_across, right), hop(6, n_across, left)
    g6.start()
    g7.start()

    @pl.loop(0, chunks)
    def _(p):
        load_cross(p).wait()

        @pl.when(p + 1 < chunks)
        def _():
            load_cross(p + 1).start()

        high, low = split(xstage[p % 2])
        xhi[p] = high
        xlo[p] = low

    slots = NROW * CAP
    group = 2 * PAD
    for s in range(2):
        for g in range(4):
            place = (lax.broadcasted_iota(jnp.int32, (group, slots), 0) + g * group).astype(F32)
            hit = jnp.where(place == tgt[s : s + 1, 0:slots], 1.0, 0.0)
            onehot[s, g] = hit.astype(BF16)

    for i in range(7):
        remote(meta.at[r], mrecv.at[row_src(i)], ms.at[i], mr.at[i], (row_src(i), c)).wait_recv()
    diagonal = lax.broadcasted_iota(jnp.int32, (CAP, 128), 0) == lax.broadcasted_iota(jnp.int32, (CAP, 128), 1)
    for s in range(NROW):
        for row, target in ((0, colb), (1, colc)):
            column = jnp.sum(jnp.where(diagonal, mrecv[s, row : row + 1, :], 0.0), axis=1, keepdims=True)
            target[s * CAP : (s + 1) * CAP, :] = jnp.broadcast_to(column, (CAP, 128))

    def take(g, first):
        high, low = split(gath[pl.ds(g * 2, 2)].reshape(group, width))
        ahi[g] = high
        alo[g] = low
        place = (lax.broadcasted_iota(jnp.int32, (slots, group), 1) + g * group).astype(F32)
        chosen = jnp.where(place == colb[:, 0:1], 1.0, 0.0).astype(BF16)
        for n in range(chunks):
            columns = slice(n * CHUNK, (n + 1) * CHUNK)
            part = dot(chosen, ahi[g, :, columns]) + dot(chosen, alo[g, :, columns])
            if first:
                pacc[:, columns] = part
            else:
                pacc[:, columns] += part

    take(x, True)
    n_far = x2 * 2 + yh
    hop(3, n_far, right, 0).wait_recv()
    hop(4, n_far, left, half).wait_recv()
    g8 = hop(7, n_far, across)
    g8.start()
    hop(5, xm1 * 2 + 1 - yh, right).wait_recv()
    take(xm1, False)
    hop(6, xp * 2 + 1 - yh, left).wait_recv()
    take(xp, False)
    hop(7, x2 * 2 + 1 - yh, across).wait_recv()
    take(x2, False)
    for n in range(chunks):
        columns = slice(n * CHUNK, (n + 1) * CHUNK)
        high, low = split(pacc[:, columns] * colc[:, 0:1])
        phi[:, columns] = high
        plo[:, columns] = low

    def returned(k, i, source):
        return remote(cross.at[k, source], back.at[k, r], ts.at[k, i], tr.at[k, i], (source, c))

    def product(k):
        value = dot(phi[...], xhi[k]) + dot(plo[...], xhi[k]) + dot(phi[...], xlo[k])
        cross[k] = value.reshape(NROW, CAP, CHUNK)
        for i in range(7):
            returned(k, i, row_dev(i)).start()
        back[k, r] = cross[k, r]

    def ladder(s, k, target):
        p = s * chunks + k

        @pl.loop(0, 4)
        def _(g):
            value = dot_t(ahi[g], chi[p]) + dot_t(alo[g], chi[p]) + dot_t(ahi[g], clo[p])
            target[pl.ds(g * 2, 2)] = value.reshape(2, PAD, CHUNK)

    def scatter(s, k, target):
        high, low = split(back[k].reshape(slots, CHUNK))

        @pl.loop(0, 4)
        def _(g):
            value = dot(onehot[s, g], high) + dot(onehot[s, g], low)
            target[pl.ds(g * 2, 2)] += value.reshape(2, PAD, CHUNK)

    def to_sibling(k):
        return remote(sib.at[k % 2], crecv.at[k], cs.at[k], cr.at[k], sibling)

    def unit(k, depth, side):
        return mine.at[k, side * 4 + depth]

    def around(k, i):
        sources = [
            (unit(k, z2, 0), above),
            (unit(k, z2, 1), below),
            (unit(k, zp, 1), above),
            (unit(k, zm, 0), below),
            (unit(k, zp, 0), above),
            (unit(k, zm, 1), below),
        ]
        return remote(sources[i][0], zrecv.at[k, i], zs.at[k, i], zr.at[k, i], sources[i][1])

    def aside(k):
        return remote(unit(k, z, 1 - yl), yrecv.at[k], ys.at[k], yr.at[k], beside)

    def exchange(k):
        return remote(esend.at[k], erecv.at[k], es.at[k], er.at[k], sibling)

    product(0)
    block = rows // 2

    @pl.loop(0, chunks + 4)
    def _(t):
        @pl.when(t < chunks)
        def _():
            @pl.when(t + 1 < chunks)
            def _():
                product(t + 1)

            @pl.when(t >= 2)
            def _():
                to_sibling(t - 2).wait_send()

            ladder(1 - core, t, sib.at[t % 2])
            for i in range(7):
                remote(
                    cross.at[t, r], back.at[t, row_src(i)], ts.at[t, i], tr.at[t, i], (row_src(i), c)
                ).wait_recv()
            scatter(1 - core, t, sib.at[t % 2])
            to_sibling(t).start()
            ladder(core, t, mine.at[t])
            scatter(core, t, mine.at[t])
            to_sibling(t).wait_recv()
            mine[t] += crecv[t]
            for i in range(4):
                around(t, i).start()

        @pl.when((t >= 1) & (t < chunks + 1))
        def _():
            k = t - 1
            around(k, 0).wait_recv()
            mine[k, zp] += zrecv[k, 0]
            around(k, 4).start()
            around(k, 1).wait_recv()
            mine[k, 4 + zm] += zrecv[k, 1]
            around(k, 5).start()

        @pl.when((t >= 2) & (t < chunks + 2))
        def _():
            k = t - 2
            for i in range(2, 6):
                around(k, i).wait_recv()
            mine[k, z] += zrecv[k, 3] + zrecv[k, 4]
            mine[k, 4 + z] += zrecv[k, 2] + zrecv[k, 5]
            aside(k).start()

        @pl.when((t >= 3) & (t < chunks + 3))
        def _():
            k = t - 3
            aside(k).wait_recv()
            mine[k, yl * 4 + z] += yrecv[k]
            low = mine[k, yl * 4 + z, 0:block, :]
            high = mine[k, yl * 4 + z, block:rows, :]
            esend[k] = jnp.where(core == 0, high, low)
            exchange(k).start()
            out[:, pl.ds(pl.multiple_of(core * width + k * CHUNK, CHUNK), CHUNK)] = jnp.where(core == 0, low, high)

        @pl.when(t >= 4)
        def _():
            k = t - 4
            exchange(k).wait_recv()
            out[:, pl.ds(pl.multiple_of((1 - core) * width + k * CHUNK, CHUNK), CHUNK)] = erecv[k]

    for copy in [g1, g2, g3, g4, g5, g6, g7, g8] + mcopies:
        copy.wait_send()

    @pl.loop(0, chunks)
    def _(k):
        for i in range(7):
            returned(k, i, row_dev(i)).wait_send()
        for i in range(6):
            around(k, i).wait_send()
        aside(k).wait_send()
        exchange(k).wait_send()

    to_sibling(chunks - 2).wait_send()
    to_sibling(chunks - 1).wait_send()


def tables(channel_slot, channel_of, source_row, target_row, recoupling, shard):
    names = jnp.arange(NROW, dtype=jnp.int32)
    named = channel_of[0] == names[None, :]
    owners = jnp.sum(jnp.where(named, channel_slot[None, :], 0), axis=1)
    marks = (owners[:, None] == names[None, :]).astype(jnp.int32)
    before = jnp.cumsum(marks, axis=0) - marks
    slot = owners * CAP + jnp.sum(before * marks, axis=1)
    match = slot[None, :] == jnp.arange(NROW * CAP, dtype=jnp.int32)[:, None]
    pad = PAD - shard
    source = source_row[0] + pad * (source_row[0] // shard)
    hole = target_row[0] // 2
    hole = hole + pad * (hole // shard)
    odd = target_row[0] % 2

    def place(value, where):
        return (jnp.sum(jnp.where(where, value[None, :] + 1, 0), axis=1) - 1).astype(F32)

    chosen = place(source, match)
    scale = jnp.sum(jnp.where(match, recoupling[0][None, :], 0.0), axis=1)
    even_target = place(hole, match & (odd == 0)[None, :])
    odd_target = place(hole, match & (odd == 1)[None, :])
    meta = jnp.stack([chosen.reshape(NROW, CAP), scale.reshape(NROW, CAP)], axis=1)
    meta = jnp.pad(meta, ((0, 0), (0, 6), (0, 128 - CAP)))
    return meta, jnp.stack([even_target, odd_target])


def on_device(
    amplitude,
    ladder_coupling,
    crossed_coupling,
    channel_slot,
    channel_of,
    source_row,
    target_row,
    recoupling,
    driving,
    denominator,
):
    rows, width = amplitude.shape
    chunks = width // CHUNK
    slots = NROW * CAP
    group = 2 * PAD
    meta, tgt = tables(channel_slot, channel_of, source_row, target_row, recoupling, rows)
    dma = pltpu.SemaphoreType.DMA
    vmem = pltpu.VMEM
    summed = pl.pallas_call(
        kernel,
        out_shape=jax.ShapeDtypeStruct((rows // 2, 2 * width), F32),
        in_specs=[pl.BlockSpec(memory_space=pltpu.VMEM)] * 2 + [pl.BlockSpec(memory_space=pl.ANY)] * 3,
        out_specs=pl.BlockSpec(memory_space=pltpu.VMEM),
        scratch_shapes=[
            vmem((rows, width), F32),
            vmem((NROW, PAD, width), F32),
            vmem((4, group, width), BF16),
            vmem((4, group, width), BF16),
            vmem((2, CHUNK, width), F32),
            vmem((2 * chunks, CHUNK, width), BF16),
            vmem((2 * chunks, CHUNK, width), BF16),
            vmem((2, width, CHUNK), F32),
            vmem((chunks, width, CHUNK), BF16),
            vmem((chunks, width, CHUNK), BF16),
            vmem((NROW, 8, 128), F32),
            vmem((slots, 128), F32),
            vmem((slots, 128), F32),
            vmem((slots, width), F32),
            vmem((slots, width), BF16),
            vmem((slots, width), BF16),
            vmem((2, 4, group, slots), BF16),
            vmem((chunks, NROW, CAP, CHUNK), F32),
            vmem((chunks, NROW, CAP, CHUNK), F32),
            vmem((2, NROW, PAD, CHUNK), F32),
            vmem((chunks, NROW, PAD, CHUNK), F32),
            vmem((chunks, NROW, PAD, CHUNK), F32),
            vmem((chunks, 6, PAD, CHUNK), F32),
            vmem((chunks, PAD, CHUNK), F32),
            vmem((chunks, rows // 2, CHUNK), F32),
            vmem((chunks, rows // 2, CHUNK), F32),
            dma,
            dma((4,)),
            dma((8,)),
            dma((8,)),
            dma((7,)),
            dma((7,)),
            dma((chunks, 7)),
            dma((chunks, 7)),
            dma((chunks,)),
            dma((chunks,)),
            dma((chunks, 6)),
            dma((chunks, 6)),
            dma((chunks,)),
            dma((chunks,)),
            dma((chunks,)),
            dma((chunks,)),
        ],
        compiler_params=pltpu.CompilerParams(
            collective_id=0, has_side_effects=True, vmem_limit_bytes=63 * 1024 * 1024
        ),
        cost_estimate=pl.CostEstimate(flops=24_000_000_000, bytes_accessed=22_000_000, transcendentals=0),
    )(meta, tgt, amplitude, ladder_coupling, crossed_coupling)
    return (driving + summed) / denominator


def solution(mesh):
    in_specs = (
        P("row", "col"),
        P("row", "col"),
        P("row", None, None),
        P(),
        P("col", "row", None),
        P("col", "row"),
        P("col", "row"),
        P("col", "row"),
        P("col", "row"),
        P("col", "row"),
    )
    out_specs = P("col", "row")
    return jax.shard_map(
        on_device, mesh=mesh, in_specs=in_specs, out_specs=out_specs, check_vma=False
    )
```

time: 299 us -> 119 us (0.40); the launches traced: 294 us -> 118 us
  Pallas kernels: 0 us -> 110 us
  waiting for transfers between devices: 96.6 us -> 0 us
  blocking collectives: 80.4 us -> 0 us
  matrix products: 48.5 us -> 0 us
  local copies, waits for them, and re-layouts: 20.1 us -> 0.19 us
  other arithmetic: 22.8 us -> 7.73 us
  between operations: 14.2 us -> 0.08 us
  starting transfers between devices: 11.3 us -> 0 us
    pallas_call x0 -> x1, Pallas kernels: none -> 110 us  [on_device(): pl.pallas_call(kernel, out_shape=jax.ShapeDtypeStruct((rows // 2, 2 * wid...]
    all_gather x1 -> x0, waiting for transfers between devices: 63.2 us -> none  [on_device(): gathered = lax.all_gather(amplitude, 'row', axis=0, tiled=True)]
    unnamed x1 -> x0, blocking collectives: 56.1 us -> none
    dot_general x2 -> x0, matrix products: 48.5 us -> none  [the longest x1 37.6 us: on_device(): lax.dot_general(gathered, ladder_coupling, (((1,), (1,)), ((), ())), prec...]
    all_to_all x1 -> x0, blocking collectives: 24.3 us -> none  [on_device(): lax.all_to_all(buffer, 'row', split_axis=0, concat_axis=0, tiled=True)]
    all_to_all x1 -> x0, waiting for transfers between devices: 21.7 us -> none  [on_device(): lax.all_to_all(mixture, 'row', split_axis=0, concat_axis=0, tiled=True)]
    unnamed x3 -> x0, waiting for transfers between devices: 11.7 us -> none
    reshape x1 -> x0, local copies, waits for them, and re-layouts: 9.83 us -> none  [on_device(): particle_hole = spread.reshape(hole_pairs, row_width)]
  transfers between devices with their start and end apart: 4 -> 0, of which waited for: 3 -> 0; matrix products, arithmetic and copies ran while one was open for 5% -> 0% of each run, Pallas kernels for 0% -> 0%
where the time goes in v1:
time: 119 us; the launch traced here: 118 us
  Pallas kernels  110 us (92%)
  other arithmetic  7.73 us (6%)
    pallas_call x1, Pallas kernels, on_device(): pl.pallas_call(kernel, out_shape=jax.ShapeDtypeStruct((rows // 2, 2 * wid...  110 us

profile of v1, /device:TPU:1, one launch (start us, length us, event | category | flops | bytes accessed | tf_op | source)
XLA Modules:
  0.0 118.5 jit_solution(2861401370083097950)
XLA Ops:
  0.0 0.8 select_reduce_fusion.5
  0.8 0.7 add_bitcast_fusion.1
  1.5 0.7 compare_bitcast_fusion
  2.2 0.7 add_bitcast_fusion
  2.9 0.1 fusion.2
  3.0 0.2 reduce_window_sum.11
  3.1 0.2 select_reduce_fusion.4
  3.3 0.8 select_reduce_fusion.2
  4.1 0.1 stack_reshape.4
  4.2 0.3 select_reduce_fusion.1
  4.5 0.6 pad_maximum_fusion.tgt
  5.1 0.1 convert_element_type.46
  5.2 0.6 select_maximum_fusion.meta
  5.9 0.0 copy-start
  5.9 110.5 %shard_map.100 = f32[50,2560]{1,0:T(8,128)} custom-call(f32[8,8,128]{2,1,0:T(8,128)} %select_maximum_fusion.meta, f32[2,320]{1,0:T(2,128)} %pad_maximum_fusion.tgt, f32[100,1280]{1,0:T(8,128)} %amp.1, f32[2560,1280]{1,0:T(8,128)} %lad.1, f32[1,1280,1280]{2,1,0:T(8,128)} %xm.1), custom_call_target="tpu_custom_call" | custom-call | flops 24000000000 | bytes 22000000 | tf_op jit(solution)/shard_map/pallas_call | solution.py:363
  116.4 0.0 copy-done
  116.4 2.1 %add_divide_fusion = f32[50,2560]{1,0:T(8,128)} fusion(f32[50,2560]{1,0:T(8,128)S(1)} %copy-done, f32[50,2560]{1,0:T(8,128)} %param.18, f32[50,2560]{1,0:T(8,128)} %shard_map.100), kind=kLoop, calls=%fused_computation | loop fusion | flops 256000 | bytes 2048000 | tf_op jit(solution)/shard_map/div | solution.py:417
  (6 shorter events, 0.0 us)
Async XLA Ops:
  5.9 110.5 %copy-start = (f32[50,2560]{1,0:T(8,128)S(1)}, f32[50,2560]{1,0:T(8,128)}, u32[]{:S(2)}) copy-start(f32[50,2560]{1,0:T(8,128)} %param.19) | copy-start | bytes 1536004

commit v2 on v1

--- a/solution.py
+++ b/solution.py
@@ -31,7 +31,7 @@
 def kernel(
     meta, tgt, amp, lad, xm, out,
     own, gath, ahi, alo, stage, chi, clo, xstage, xhi, xlo, mrecv, colb, colc, pacc, phi, plo, onehot,
-    cross, back, sib, mine, crecv, zrecv, yrecv, esend, erecv,
+    cross, back, sib, mine, crecv, zrecv, hrecv, yrecv, esend, erecv,
     lsem, stsem, gs, gr, ms, mr, ts, tr, cs, cr, zs, zr, ys, yr, es, er,
 ):
     rows, width = amp.shape
@@ -113,17 +113,75 @@
         chi[p] = high
         clo[p] = low
 
-    n_left, n_right, n_across = xm1 * 2 + yh, xp * 2 + yh, x * 2 + 1 - yh
+    slots = NROW * CAP
+    pairs = [
+        (r, x * 2 + 1 - yh),
+        (xm1 * 2 + yh, xp * 2 + yh),
+        (x2 * 2 + yh, xm1 * 2 + 1 - yh),
+        (xp * 2 + 1 - yh, x2 * 2 + 1 - yh),
+    ]
+    units = [shard for pair in pairs for shard in pair]
+    group = 2 * PAD
+
+    def place(g, shape, axis):
+        index = lax.broadcasted_iota(jnp.int32, shape, axis)
+        return jnp.where(index < PAD, index + pairs[g][0] * PAD, index + (pairs[g][1] - 1) * PAD).astype(F32)
+
+    def convert(g):
+        high, low = split(jnp.concatenate([gath[pairs[g][0]], gath[pairs[g][1]]], axis=0))
+        ahi[g] = high
+        alo[g] = low
+
+    def take(g):
+        chosen = jnp.where(place(g, (slots, group), 1) == colb[:, 0:1], 1.0, 0.0).astype(BF16)
+        for n in range(chunks):
+            columns = slice(n * CHUNK, (n + 1) * CHUNK)
+            part = dot(chosen, ahi[g, :, columns]) + dot(chosen, alo[g, :, columns])
+            if g == 0:
+                pacc[:, columns] = part
+            else:
+                pacc[:, columns] += part
+
+    def ladder(s, k, target, h):
+        p = s * chunks + k
+        high = ahi[2 * h : 2 * h + 2].reshape(2 * group, width)
+        low = alo[2 * h : 2 * h + 2].reshape(2 * group, width)
+        value = dot_t(high, chi[p]) + dot_t(low, chi[p]) + dot_t(high, clo[p])
+        for i in range(4):
+            target[units[4 * h + i]] = value[i * PAD : (i + 1) * PAD]
+
+    def early(k):
+        ladder(1 - core, k, sib.at[k], 0)
+        ladder(core, k, mine.at[k], 0)
+
+    n_left, n_right, n_across, n_far = xm1 * 2 + yh, xp * 2 + yh, x * 2 + 1 - yh, x2 * 2 + yh
     hop(0, n_left, right).wait_recv()
     g4 = hop(3, n_left, right, 0)
     g4.start()
     hop(1, n_right, left).wait_recv()
     g5 = hop(4, n_right, left, half)
     g5.start()
+    convert(1)
     hop(2, n_across, across).wait_recv()
+    convert(0)
+
+    @pl.loop(0, 2)
+    def _(k):
+        early(k)
+
+    g4.wait_send()
+    g5.wait_send()
     g6, g7 = hop(5, n_across, right), hop(6, n_across, left)
     g6.start()
     g7.start()
+    hop(3, n_far, right, 0).wait_recv()
+    hop(4, n_far, left, half).wait_recv()
+    g8 = hop(7, n_far, across)
+    g8.start()
+
+    @pl.loop(2, chunks)
+    def _(k):
+        early(k)
 
     @pl.loop(0, chunks)
     def _(p):
@@ -136,14 +194,6 @@
         high, low = split(xstage[p % 2])
         xhi[p] = high
         xlo[p] = low
-
-    slots = NROW * CAP
-    group = 2 * PAD
-    for s in range(2):
-        for g in range(4):
-            place = (lax.broadcasted_iota(jnp.int32, (group, slots), 0) + g * group).astype(F32)
-            hit = jnp.where(place == tgt[s : s + 1, 0:slots], 1.0, 0.0)
-            onehot[s, g] = hit.astype(BF16)
 
     for i in range(7):
         remote(meta.at[r], mrecv.at[row_src(i)], ms.at[i], mr.at[i], (row_src(i), c)).wait_recv()
@@ -152,33 +202,20 @@
         for row, target in ((0, colb), (1, colc)):
             column = jnp.sum(jnp.where(diagonal, mrecv[s, row : row + 1, :], 0.0), axis=1, keepdims=True)
             target[s * CAP : (s + 1) * CAP, :] = jnp.broadcast_to(column, (CAP, 128))
-
-    def take(g, first):
-        high, low = split(gath[pl.ds(g * 2, 2)].reshape(group, width))
-        ahi[g] = high
-        alo[g] = low
-        place = (lax.broadcasted_iota(jnp.int32, (slots, group), 1) + g * group).astype(F32)
-        chosen = jnp.where(place == colb[:, 0:1], 1.0, 0.0).astype(BF16)
-        for n in range(chunks):
-            columns = slice(n * CHUNK, (n + 1) * CHUNK)
-            part = dot(chosen, ahi[g, :, columns]) + dot(chosen, alo[g, :, columns])
-            if first:
-                pacc[:, columns] = part
-            else:
-                pacc[:, columns] += part
-
-    take(x, True)
-    n_far = x2 * 2 + yh
-    hop(3, n_far, right, 0).wait_recv()
-    hop(4, n_far, left, half).wait_recv()
-    g8 = hop(7, n_far, across)
-    g8.start()
+    take(0)
+    take(1)
+    for s in range(2):
+        for g in range(4):
+            hit = jnp.where(place(g, (group, slots), 0) == tgt[s : s + 1, 0:slots], 1.0, 0.0)
+            onehot[s, g] = hit.astype(BF16)
+
     hop(5, xm1 * 2 + 1 - yh, right).wait_recv()
-    take(xm1, False)
+    convert(2)
+    take(2)
     hop(6, xp * 2 + 1 - yh, left).wait_recv()
-    take(xp, False)
     hop(7, x2 * 2 + 1 - yh, across).wait_recv()
-    take(x2, False)
+    convert(3)
+    take(3)
     for n in range(chunks):
         columns = slice(n * CHUNK, (n + 1) * CHUNK)
         high, low = split(pacc[:, columns] * colc[:, 0:1])
@@ -195,49 +232,43 @@
             returned(k, i, row_dev(i)).start()
         back[k, r] = cross[k, r]
 
-    def ladder(s, k, target):
-        p = s * chunks + k
-
-        @pl.loop(0, 4)
-        def _(g):
-            value = dot_t(ahi[g], chi[p]) + dot_t(alo[g], chi[p]) + dot_t(ahi[g], clo[p])
-            target[pl.ds(g * 2, 2)] = value.reshape(2, PAD, CHUNK)
-
     def scatter(s, k, target):
         high, low = split(back[k].reshape(slots, CHUNK))
-
-        @pl.loop(0, 4)
-        def _(g):
-            value = dot(onehot[s, g], high) + dot(onehot[s, g], low)
-            target[pl.ds(g * 2, 2)] += value.reshape(2, PAD, CHUNK)
+        hits = onehot[s].reshape(4 * group, slots)
+        value = dot(hits, high) + dot(hits, low)
+        for i in range(8):
+            target[units[i]] += value[i * PAD : (i + 1) * PAD]
 
     def to_sibling(k):
-        return remote(sib.at[k % 2], crecv.at[k], cs.at[k], cr.at[k], sibling)
+        return remote(sib.at[k], crecv.at[k], cs.at[k], cr.at[k], sibling)
 
     def unit(k, depth, side):
         return mine.at[k, side * 4 + depth]
 
+    quarter = CHUNK // 2
+
     def around(k, i):
-        sources = [
-            (unit(k, z2, 0), above),
-            (unit(k, z2, 1), below),
-            (unit(k, zp, 1), above),
-            (unit(k, zm, 0), below),
-            (unit(k, zp, 0), above),
-            (unit(k, zm, 1), below),
-        ]
-        return remote(sources[i][0], zrecv.at[k, i], zs.at[k, i], zr.at[k, i], sources[i][1])
-
-    def aside(k):
-        return remote(unit(k, z, 1 - yl), yrecv.at[k], ys.at[k], yr.at[k], beside)
+        source, target, device = [
+            (unit(k, zp, 1 - yl), zrecv.at[k, 0], above),
+            (unit(k, zm, 1 - yl), zrecv.at[k, 1], below),
+            (unit(k, z2, yl).at[:, 0:quarter], hrecv.at[k, 0], above),
+            (unit(k, z2, yl).at[:, quarter:CHUNK], hrecv.at[k, 1], below),
+            (unit(k, zp, yl), zrecv.at[k, 2], above),
+            (unit(k, zm, yl), zrecv.at[k, 3], below),
+        ][i]
+        return remote(source, target, zs.at[k, i], zr.at[k, i], device)
+
+    def aside(k, i):
+        return remote(unit(k, z if i else z2, 1 - yl), yrecv.at[k, i], ys.at[k, i], yr.at[k, i], beside)
 
     def exchange(k):
         return remote(esend.at[k], erecv.at[k], es.at[k], er.at[k], sibling)
 
     product(0)
     block = rows // 2
-
-    @pl.loop(0, chunks + 4)
+    same, other = yl * 4, (1 - yl) * 4
+
+    @pl.loop(0, chunks + 3)
     def _(t):
         @pl.when(t < chunks)
         def _():
@@ -245,74 +276,78 @@
             def _():
                 product(t + 1)
 
-            @pl.when(t >= 2)
-            def _():
-                to_sibling(t - 2).wait_send()
-
-            ladder(1 - core, t, sib.at[t % 2])
+            ladder(1 - core, t, sib.at[t], 1)
             for i in range(7):
                 remote(
                     cross.at[t, r], back.at[t, row_src(i)], ts.at[t, i], tr.at[t, i], (row_src(i), c)
                 ).wait_recv()
-            scatter(1 - core, t, sib.at[t % 2])
+            scatter(1 - core, t, sib.at[t])
             to_sibling(t).start()
-            ladder(core, t, mine.at[t])
+
+        @pl.when((t >= 1) & (t < chunks + 1))
+        def _():
+            k = t - 1
+            aside(k, 0).wait_recv()
+            mine[k, same + z2] += yrecv[k, 0]
+            around(k, 2).start()
+            around(k, 3).start()
+
+        @pl.when(t < chunks)
+        def _():
+            ladder(core, t, mine.at[t], 1)
             scatter(core, t, mine.at[t])
             to_sibling(t).wait_recv()
             mine[t] += crecv[t]
-            for i in range(4):
-                around(t, i).start()
+            aside(t, 0).start()
+            around(t, 0).start()
+            around(t, 1).start()
 
         @pl.when((t >= 1) & (t < chunks + 1))
         def _():
             k = t - 1
+            around(k, 2).wait_recv()
+            mine[k, same + zp, :, 0:quarter] += hrecv[k, 0]
+            around(k, 4).start()
+            around(k, 3).wait_recv()
+            mine[k, same + zm, :, quarter:CHUNK] += hrecv[k, 1]
+            around(k, 5).start()
             around(k, 0).wait_recv()
-            mine[k, zp] += zrecv[k, 0]
-            around(k, 4).start()
             around(k, 1).wait_recv()
-            mine[k, 4 + zm] += zrecv[k, 1]
-            around(k, 5).start()
+            mine[k, other + z] += zrecv[k, 0] + zrecv[k, 1]
+            aside(k, 1).start()
 
         @pl.when((t >= 2) & (t < chunks + 2))
         def _():
             k = t - 2
-            for i in range(2, 6):
-                around(k, i).wait_recv()
-            mine[k, z] += zrecv[k, 3] + zrecv[k, 4]
-            mine[k, 4 + z] += zrecv[k, 2] + zrecv[k, 5]
-            aside(k).start()
-
-        @pl.when((t >= 3) & (t < chunks + 3))
-        def _():
-            k = t - 3
-            aside(k).wait_recv()
-            mine[k, yl * 4 + z] += yrecv[k]
-            low = mine[k, yl * 4 + z, 0:block, :]
-            high = mine[k, yl * 4 + z, block:rows, :]
+            around(k, 4).wait_recv()
+            around(k, 5).wait_recv()
+            aside(k, 1).wait_recv()
+            mine[k, same + z] += zrecv[k, 2] + zrecv[k, 3] + yrecv[k, 1]
+            low = mine[k, same + z, 0:block, :]
+            high = mine[k, same + z, block:rows, :]
             esend[k] = jnp.where(core == 0, high, low)
             exchange(k).start()
             out[:, pl.ds(pl.multiple_of(core * width + k * CHUNK, CHUNK), CHUNK)] = jnp.where(core == 0, low, high)
 
-        @pl.when(t >= 4)
-        def _():
-            k = t - 4
+        @pl.when(t >= 3)
+        def _():
+            k = t - 3
             exchange(k).wait_recv()
             out[:, pl.ds(pl.multiple_of((1 - core) * width + k * CHUNK, CHUNK), CHUNK)] = erecv[k]
 
-    for copy in [g1, g2, g3, g4, g5, g6, g7, g8] + mcopies:
+    for copy in [g1, g2, g3, g6, g7, g8] + mcopies:
         copy.wait_send()
 
     @pl.loop(0, chunks)
     def _(k):
         for i in range(7):
             returned(k, i, row_dev(i)).wait_send()
+        to_sibling(k).wait_send()
         for i in range(6):
             around(k, i).wait_send()
-        aside(k).wait_send()
+        aside(k, 0).wait_send()
+        aside(k, 1).wait_send()
         exchange(k).wait_send()
-
-    to_sibling(chunks - 2).wait_send()
-    to_sibling(chunks - 1).wait_send()
 
 
 def tables(channel_slot, channel_of, source_row, target_row, recoupling, shard):
@@ -385,11 +420,12 @@
             vmem((2, 4, group, slots), BF16),
             vmem((chunks, NROW, CAP, CHUNK), F32),
             vmem((chunks, NROW, CAP, CHUNK), F32),
-            vmem((2, NROW, PAD, CHUNK), F32),
             vmem((chunks, NROW, PAD, CHUNK), F32),
             vmem((chunks, NROW, PAD, CHUNK), F32),
-            vmem((chunks, 6, PAD, CHUNK), F32),
-            vmem((chunks, PAD, CHUNK), F32),
+            vmem((chunks, NROW, PAD, CHUNK), F32),
+            vmem((chunks, 4, PAD, CHUNK), F32),
+            vmem((chunks, 2, PAD, CHUNK // 2), F32),
+            vmem((chunks, 2, PAD, CHUNK), F32),
             vmem((chunks, rows // 2, CHUNK), F32),
             vmem((chunks, rows // 2, CHUNK), F32),
             dma,
@@ -404,8 +440,8 @@
             dma((chunks,)),
             dma((chunks, 6)),
             dma((chunks, 6)),
-            dma((chunks,)),
-            dma((chunks,)),
+            dma((chunks, 2)),
+            dma((chunks, 2)),
             dma((chunks,)),
             dma((chunks,)),
         ],

time: 119 us -> 113 us (0.950)
  Pallas kernels: 110 us -> 105 us
    pallas_call x1, Pallas kernels: 110 us -> 105 us  [on_device(): pl.pallas_call(kernel, out_shape=jax.ShapeDtypeStruct((rows // 2, 2 * wid...]
where the time goes in v2:
time: 113 us
  Pallas kernels  105 us (93%)
  other arithmetic  7.73 us (7%)
    pallas_call x1, Pallas kernels, on_device(): pl.pallas_call(kernel, out_shape=jax.ShapeDtypeStruct((rows // 2, 2 * wid...  105 us

profile of v2, /device:TPU:1, one launch (start us, length us, event | category | flops | bytes accessed | tf_op | source)
XLA Modules:
  0.0 112.8 jit_solution(16381458634513142732)
XLA Ops:
  0.0 0.8 select_reduce_fusion.5
  0.8 0.7 add_bitcast_fusion.1
  1.5 0.7 compare_bitcast_fusion
  2.2 0.7 add_bitcast_fusion
  2.9 0.1 fusion.2
  3.0 0.2 reduce_window_sum.11
  3.1 0.2 select_reduce_fusion.4
  3.3 0.8 select_reduce_fusion.2
  4.1 0.1 stack_reshape.4
  4.2 0.3 select_reduce_fusion.1
  4.5 0.6 pad_maximum_fusion.tgt
  5.1 0.1 convert_element_type.46
  5.2 0.6 select_maximum_fusion.meta
  5.9 0.0 copy-start
  5.9 104.8 %shard_map.100 = f32[50,2560]{1,0:T(8,128)} custom-call(f32[8,8,128]{2,1,0:T(8,128)} %select_maximum_fusion.meta, f32[2,320]{1,0:T(2,128)} %pad_maximum_fusion.tgt, f32[100,1280]{1,0:T(8,128)} %amp.1, f32[2560,1280]{1,0:T(8,128)} %lad.1, f32[1,1280,1280]{2,1,0:T(8,128)} %xm.1), custom_call_target="tpu_custom_call" | custom-call | flops 24000000000 | bytes 22000000 | tf_op jit(solution)/shard_map/pallas_call | solution.py:398
  110.7 0.0 copy-done
  110.7 2.1 %add_divide_fusion = f32[50,2560]{1,0:T(8,128)} fusion(f32[50,2560]{1,0:T(8,128)S(1)} %copy-done, f32[50,2560]{1,0:T(8,128)} %param.18, f32[50,2560]{1,0:T(8,128)} %shard_map.100), kind=kLoop, calls=%fused_computation | loop fusion | flops 256000 | bytes 2048000 | tf_op jit(solution)/shard_map/div | solution.py:453
  (6 shorter events, 0.0 us)
Async XLA Ops:
  5.9 104.8 %copy-start = (f32[50,2560]{1,0:T(8,128)S(1)}, f32[50,2560]{1,0:T(8,128)}, u32[]{:S(2)}) copy-start(f32[50,2560]{1,0:T(8,128)} %param.19) | copy-start | bytes 1536004

commit v3 on v2

--- a/solution.py
+++ b/solution.py
@@ -29,10 +29,10 @@
 
 
 def kernel(
-    meta, tgt, amp, lad, xm, out,
-    own, gath, ahi, alo, stage, chi, clo, xstage, xhi, xlo, mrecv, colb, colc, pacc, phi, plo, onehot,
-    cross, back, sib, mine, crecv, zrecv, hrecv, yrecv, esend, erecv,
-    lsem, stsem, gs, gr, ms, mr, ts, tr, cs, cr, zs, zr, ys, yr, es, er,
+    channel_slot, channel_of, source_row, target_row, recoupling, amp, lad, xm, driving, denominator, out,
+    own, gath, ahi, alo, stage, chi, clo, xstage, xhi, xlo, meta, mrecv, tgt, tsib, tall, colb, colc, pacc, phi, plo,
+    onehot, cross, back, bsib, sib, mine, crecv, zrecv, yrecv, esend, erecv, drv, den,
+    lsem, stsem, gs, gr, ms, mr, ts, tr, bs, br, cs, cr, zs, zr, ys, yr, es, er,
 ):
     rows, width = amp.shape
     chunks = width // CHUNK
@@ -72,10 +72,14 @@
             xm.at[0, :, pl.ds(pl.multiple_of(p * CHUNK, CHUNK), CHUNK)], xstage.at[p % 2], stsem.at[2 + p % 2]
         )
 
-    load_own = pltpu.make_async_copy(amp, own, lsem)
+    load_own = pltpu.make_async_copy(amp, own, lsem.at[0])
+    load_drv = pltpu.make_async_copy(driving, drv, lsem.at[1])
+    load_den = pltpu.make_async_copy(denominator, den, lsem.at[2])
     load_own.start()
     load_ladder(0).start()
     load_cross(0).start()
+    load_drv.start()
+    load_den.start()
 
     barrier = pltpu.get_barrier_semaphore()
     partners = [(row_dev(i), c) for i in range(7)] + [sibling, above, below, beside]
@@ -84,6 +88,7 @@
     load_own.wait()
     gath[r, 0:rows, :] = own[...]
     gath[r, rows:PAD, :] = jnp.zeros((PAD - rows, width), F32)
+    tables(rows, channel_slot, channel_of, source_row, target_row, recoupling, meta, tgt)
     pl.semaphore_wait(barrier, len(partners))
 
     def hop(i, shard, device, columns=None):
@@ -99,6 +104,8 @@
         copy = remote(meta.at[row_dev(i)], mrecv.at[r], ms.at[i], mr.at[i], (row_dev(i), c))
         copy.start()
         mcopies.append(copy)
+    tcopy = remote(tgt, tsib, ms.at[7], mr.at[7], sibling)
+    tcopy.start()
     mrecv[r] = meta[r]
 
     @pl.loop(0, 2 * chunks)
@@ -150,9 +157,9 @@
         for i in range(4):
             target[units[4 * h + i]] = value[i * PAD : (i + 1) * PAD]
 
-    def early(k):
-        ladder(1 - core, k, sib.at[k], 0)
-        ladder(core, k, mine.at[k], 0)
+    def both(k, h):
+        ladder(1 - core, k, sib.at[k], h)
+        ladder(core, k, mine.at[k], h)
 
     n_left, n_right, n_across, n_far = xm1 * 2 + yh, xp * 2 + yh, x * 2 + 1 - yh, x2 * 2 + yh
     hop(0, n_left, right).wait_recv()
@@ -167,7 +174,7 @@
 
     @pl.loop(0, 2)
     def _(k):
-        early(k)
+        both(k, 0)
 
     g4.wait_send()
     g5.wait_send()
@@ -181,7 +188,7 @@
 
     @pl.loop(2, chunks)
     def _(k):
-        early(k)
+        both(k, 0)
 
     @pl.loop(0, chunks)
     def _(p):
@@ -204,10 +211,12 @@
             target[s * CAP : (s + 1) * CAP, :] = jnp.broadcast_to(column, (CAP, 128))
     take(0)
     take(1)
-    for s in range(2):
-        for g in range(4):
-            hit = jnp.where(place(g, (group, slots), 0) == tgt[s : s + 1, 0:slots], 1.0, 0.0)
-            onehot[s, g] = hit.astype(BF16)
+    tcopy.wait_recv()
+    tall[:, 0:slots] = tgt[pl.ds(core, 1), :]
+    tall[:, slots : 2 * slots] = tsib[pl.ds(core, 1), :]
+    for g in range(4):
+        hit = jnp.where(place(g, (group, 2 * slots), 0) == tall[...], 1.0, 0.0)
+        onehot[g] = hit.astype(BF16)
 
     hop(5, xm1 * 2 + 1 - yh, right).wait_recv()
     convert(2)
@@ -232,12 +241,12 @@
             returned(k, i, row_dev(i)).start()
         back[k, r] = cross[k, r]
 
-    def scatter(s, k, target):
-        high, low = split(back[k].reshape(slots, CHUNK))
-        hits = onehot[s].reshape(4 * group, slots)
+    def scatter(k):
+        high, low = split(jnp.concatenate([back[k].reshape(slots, CHUNK), bsib[k].reshape(slots, CHUNK)], axis=0))
+        hits = onehot[...].reshape(4 * group, 2 * slots)
         value = dot(hits, high) + dot(hits, low)
         for i in range(8):
-            target[units[i]] += value[i * PAD : (i + 1) * PAD]
+            mine[k, units[i]] += value[i * PAD : (i + 1) * PAD] + crecv[k, units[i]]
 
     def to_sibling(k):
         return remote(sib.at[k], crecv.at[k], cs.at[k], cr.at[k], sibling)
@@ -245,97 +254,106 @@
     def unit(k, depth, side):
         return mine.at[k, side * 4 + depth]
 
-    quarter = CHUNK // 2
+    def pass_on(k):
+        return remote(back.at[k], bsib.at[k], bs.at[k], br.at[k], sibling)
 
     def around(k, i):
-        source, target, device = [
-            (unit(k, zp, 1 - yl), zrecv.at[k, 0], above),
-            (unit(k, zm, 1 - yl), zrecv.at[k, 1], below),
-            (unit(k, z2, yl).at[:, 0:quarter], hrecv.at[k, 0], above),
-            (unit(k, z2, yl).at[:, quarter:CHUNK], hrecv.at[k, 1], below),
-            (unit(k, zp, yl), zrecv.at[k, 2], above),
-            (unit(k, zm, yl), zrecv.at[k, 3], below),
+        source, device = [
+            (unit(k, z2, 0), above),
+            (unit(k, z2, 1), below),
+            (unit(k, zp, 1), above),
+            (unit(k, zm, 0), below),
+            (unit(k, zp, 0), above),
+            (unit(k, zm, 1), below),
         ][i]
-        return remote(source, target, zs.at[k, i], zr.at[k, i], device)
-
-    def aside(k, i):
-        return remote(unit(k, z if i else z2, 1 - yl), yrecv.at[k, i], ys.at[k, i], yr.at[k, i], beside)
+        return remote(source, zrecv.at[k, i], zs.at[k, i], zr.at[k, i], device)
+
+    def aside(k):
+        return remote(unit(k, z, 1 - yl), yrecv.at[k], ys.at[k], yr.at[k], beside)
 
     def exchange(k):
         return remote(esend.at[k], erecv.at[k], es.at[k], er.at[k], sibling)
 
+    def solve(k, half_index, value):
+        columns = pl.ds(pl.multiple_of(half_index * width + k * CHUNK, CHUNK), CHUNK)
+        out[:, columns] = (drv[:, columns] + value) / den[:, columns]
+
+    def late(k):
+        ladder(1 - core, k, sib.at[k], 1)
+        to_sibling(k).start()
+        ladder(core, k, mine.at[k], 1)
+
     product(0)
+    product(1)
+    late(0)
+    load_drv.wait()
+    load_den.wait()
     block = rows // 2
-    same, other = yl * 4, (1 - yl) * 4
-
-    @pl.loop(0, chunks + 3)
+    final = yl * 4 + z
+
+    @pl.loop(0, chunks + 4)
     def _(t):
         @pl.when(t < chunks)
         def _():
-            @pl.when(t + 1 < chunks)
-            def _():
-                product(t + 1)
-
-            ladder(1 - core, t, sib.at[t], 1)
             for i in range(7):
                 remote(
                     cross.at[t, r], back.at[t, row_src(i)], ts.at[t, i], tr.at[t, i], (row_src(i), c)
                 ).wait_recv()
-            scatter(1 - core, t, sib.at[t])
-            to_sibling(t).start()
+            pass_on(t).start()
+
+            @pl.when(t + 2 < chunks)
+            def _():
+                product(t + 2)
+
+        @pl.when(t + 1 < chunks)
+        def _():
+            late(t + 1)
+
+        @pl.when(t < chunks)
+        def _():
+            to_sibling(t).wait_recv()
+            pass_on(t).wait_recv()
+            scatter(t)
+            for i in range(4):
+                around(t, i).start()
 
         @pl.when((t >= 1) & (t < chunks + 1))
         def _():
             k = t - 1
-            aside(k, 0).wait_recv()
-            mine[k, same + z2] += yrecv[k, 0]
-            around(k, 2).start()
-            around(k, 3).start()
-
-        @pl.when(t < chunks)
-        def _():
-            ladder(core, t, mine.at[t], 1)
-            scatter(core, t, mine.at[t])
-            to_sibling(t).wait_recv()
-            mine[t] += crecv[t]
-            aside(t, 0).start()
-            around(t, 0).start()
-            around(t, 1).start()
-
-        @pl.when((t >= 1) & (t < chunks + 1))
-        def _():
-            k = t - 1
-            around(k, 2).wait_recv()
-            mine[k, same + zp, :, 0:quarter] += hrecv[k, 0]
+            around(k, 0).wait_recv()
+            mine[k, zp] += zrecv[k, 0]
             around(k, 4).start()
-            around(k, 3).wait_recv()
-            mine[k, same + zm, :, quarter:CHUNK] += hrecv[k, 1]
+            around(k, 1).wait_recv()
+            mine[k, 4 + zm] += zrecv[k, 1]
             around(k, 5).start()
-            around(k, 0).wait_recv()
-            around(k, 1).wait_recv()
-            mine[k, other + z] += zrecv[k, 0] + zrecv[k, 1]
-            aside(k, 1).start()
 
         @pl.when((t >= 2) & (t < chunks + 2))
         def _():
             k = t - 2
-            around(k, 4).wait_recv()
-            around(k, 5).wait_recv()
-            aside(k, 1).wait_recv()
-            mine[k, same + z] += zrecv[k, 2] + zrecv[k, 3] + yrecv[k, 1]
-            low = mine[k, same + z, 0:block, :]
-            high = mine[k, same + z, block:rows, :]
+            for i in range(2, 6):
+                around(k, i).wait_recv()
+            mine[k, z] += zrecv[k, 3] + zrecv[k, 4]
+            mine[k, 4 + z] += zrecv[k, 2] + zrecv[k, 5]
+            aside(k).start()
+
+        @pl.when((t >= 3) & (t < chunks + 3))
+        def _():
+            k = t - 3
+            aside(k).wait_recv()
+            mine[k, final] += yrecv[k]
+            low = mine[k, final, 0:block, :]
+            high = mine[k, final, block:rows, :]
             esend[k] = jnp.where(core == 0, high, low)
             exchange(k).start()
-            out[:, pl.ds(pl.multiple_of(core * width + k * CHUNK, CHUNK), CHUNK)] = jnp.where(core == 0, low, high)
-
-        @pl.when(t >= 3)
-        def _():
-            k = t - 3
+            solve(k, core, jnp.where(core == 0, low, high))
+
+        @pl.when(t >= 4)
+        def _():
+            k = t - 4
             exchange(k).wait_recv()
-            out[:, pl.ds(pl.multiple_of((1 - core) * width + k * CHUNK, CHUNK), CHUNK)] = erecv[k]
-
-    for copy in [g1, g2, g3, g6, g7, g8] + mcopies:
+            solve(k, 1 - core, erecv[k])
+
+    for copy in [g1, g2, g3, g6, g7, g8, tcopy] + mcopies:
         copy.wait_send()
 
     @pl.loop(0, chunks)
@@ -345,35 +363,47 @@
         to_sibling(k).wait_send()
         for i in range(6):
             around(k, i).wait_send()
-        aside(k, 0).wait_send()
-        aside(k, 1).wait_send()
+        aside(k).wait_send()
+        pass_on(k).wait_send()
         exchange(k).wait_send()
 
 
-def tables(channel_slot, channel_of, source_row, target_row, recoupling, shard):
-    names = jnp.arange(NROW, dtype=jnp.int32)
-    named = channel_of[0] == names[None, :]
-    owners = jnp.sum(jnp.where(named, channel_slot[None, :], 0), axis=1)
-    marks = (owners[:, None] == names[None, :]).astype(jnp.int32)
-    before = jnp.cumsum(marks, axis=0) - marks
-    slot = owners * CAP + jnp.sum(before * marks, axis=1)
-    match = slot[None, :] == jnp.arange(NROW * CAP, dtype=jnp.int32)[:, None]
-    pad = PAD - shard
-    source = source_row[0] + pad * (source_row[0] // shard)
-    hole = target_row[0] // 2
-    hole = hole + pad * (hole // shard)
-    odd = target_row[0] % 2
-
-    def place(value, where):
-        return (jnp.sum(jnp.where(where, value[None, :] + 1, 0), axis=1) - 1).astype(F32)
-
-    chosen = place(source, match)
-    scale = jnp.sum(jnp.where(match, recoupling[0][None, :], 0.0), axis=1)
-    even_target = place(hole, match & (odd == 0)[None, :])
-    odd_target = place(hole, match & (odd == 1)[None, :])
-    meta = jnp.stack([chosen.reshape(NROW, CAP), scale.reshape(NROW, CAP)], axis=1)
-    meta = jnp.pad(meta, ((0, 0), (0, 6), (0, 128 - CAP)))
-    return meta, jnp.stack([even_target, odd_target])
+def tables(shard, channel_slot, channel_of, source_row, target_row, recoupling, meta, tgt):
+    items = channel_of.shape[1]
+    channel = channel_of[...]
+    owner = jnp.zeros(channel.shape, jnp.int32)
+    for i in range(NROW):
+        owner = jnp.where(channel == i, channel_slot[i], owner)
+    marks = jnp.where(lax.broadcasted_iota(jnp.int32, (NROW, items), 0) == owner, 1.0, 0.0)
+    square = (items, items)
+    down, along = lax.broadcasted_iota(jnp.int32, square, 0), lax.broadcasted_iota(jnp.int32, square, 1)
+    before = dot(marks.astype(BF16), jnp.where(down < along, 1.0, 0.0).astype(BF16))
+    slot = owner.astype(F32) * CAP + jnp.sum(marks * before, axis=0, keepdims=True)
+
+    def padded(row):
+        passed = row
+        for i in range(1, NROW):
+            passed = passed + jnp.where(row >= i * shard, PAD - shard, 0)
+        return passed.astype(F32)
+
+    def column(row):
+        return jnp.sum(jnp.where(down == along, row, 0.0), axis=1, keepdims=True)
+
+    target = target_row[...]
+    slot_c, scale_c = column(slot), column(recoupling[...])
+    source_c, hole_c = column(padded(source_row[...])), column(padded(target >> 1))
+    odd_c = column((target & 1).astype(F32))
+    lanes = along.astype(F32)
+    for i in range(NROW):
+        match = slot_c == lanes + i * CAP
+        meta[i, 0:1, :] = jnp.sum(jnp.where(match, source_c + 1.0, 0.0), axis=0, keepdims=True) - 1.0
+        meta[i, 1:2, :] = jnp.sum(jnp.where(match, scale_c, 0.0), axis=0, keepdims=True)
+        meta[i, 2:8, :] = jnp.zeros((6, items), F32)
+    slots = NROW * CAP
+    match = slot_c == lax.broadcasted_iota(jnp.int32, (items, slots), 1).astype(F32)
+    for i in range(2):
+        hit = match & (odd_c == float(i))
+        tgt[i : i + 1, :] = jnp.sum(jnp.where(hit, hole_c + 1.0, 0.0), axis=0, keepdims=True) - 1.0
 
 
 def on_device(
@@ -392,13 +422,14 @@
     chunks = width // CHUNK
     slots = NROW * CAP
     group = 2 * PAD
-    meta, tgt = tables(channel_slot, channel_of, source_row, target_row, recoupling, rows)
     dma = pltpu.SemaphoreType.DMA
     vmem = pltpu.VMEM
-    summed = pl.pallas_call(
+    return pl.pallas_call(
         kernel,
         out_shape=jax.ShapeDtypeStruct((rows // 2, 2 * width), F32),
-        in_specs=[pl.BlockSpec(memory_space=pltpu.VMEM)] * 2 + [pl.BlockSpec(memory_space=pl.ANY)] * 3,
+        in_specs=[pl.BlockSpec(memory_space=pltpu.SMEM)]
+        + [pl.BlockSpec(memory_space=pltpu.VMEM)] * 4
+        + [pl.BlockSpec(memory_space=pl.ANY)] * 5,
         out_specs=pl.BlockSpec(memory_space=pltpu.VMEM),
         scratch_shapes=[
             vmem((rows, width), F32),
@@ -412,36 +443,44 @@
             vmem((chunks, width, CHUNK), BF16),
             vmem((chunks, width, CHUNK), BF16),
             vmem((NROW, 8, 128), F32),
+            vmem((NROW, 8, 128), F32),
+            vmem((2, slots), F32),
+            vmem((2, slots), F32),
+            vmem((1, 2 * slots), F32),
             vmem((slots, 128), F32),
             vmem((slots, 128), F32),
             vmem((slots, width), F32),
             vmem((slots, width), BF16),
             vmem((slots, width), BF16),
-            vmem((2, 4, group, slots), BF16),
+            vmem((4, group, 2 * slots), BF16),
+            vmem((chunks, NROW, CAP, CHUNK), F32),
             vmem((chunks, NROW, CAP, CHUNK), F32),
             vmem((chunks, NROW, CAP, CHUNK), F32),
             vmem((chunks, NROW, PAD, CHUNK), F32),
             vmem((chunks, NROW, PAD, CHUNK), F32),
             vmem((chunks, NROW, PAD, CHUNK), F32),
-            vmem((chunks, 4, PAD, CHUNK), F32),
-            vmem((chunks, 2, PAD, CHUNK // 2), F32),
-            vmem((chunks, 2, PAD, CHUNK), F32),
+            vmem((chunks, 6, PAD, CHUNK), F32),
+            vmem((chunks, PAD, CHUNK), F32),
             vmem((chunks, rows // 2, CHUNK), F32),
             vmem((chunks, rows // 2, CHUNK), F32),
-            dma,
+            vmem((rows // 2, 2 * width), F32),
+            vmem((rows // 2, 2 * width), F32),
+            dma((3,)),
             dma((4,)),
             dma((8,)),
             dma((8,)),
-            dma((7,)),
-            dma((7,)),
+            dma((8,)),
+            dma((8,)),
             dma((chunks, 7)),
             dma((chunks, 7)),
             dma((chunks,)),
             dma((chunks,)),
+            dma((chunks,)),
+            dma((chunks,)),
             dma((chunks, 6)),
             dma((chunks, 6)),
-            dma((chunks, 2)),
-            dma((chunks, 2)),
+            dma((chunks,)),
+            dma((chunks,)),
             dma((chunks,)),
             dma((chunks,)),
         ],
@@ -449,8 +488,18 @@
             collective_id=0, has_side_effects=True, vmem_limit_bytes=63 * 1024 * 1024
         ),
         cost_estimate=pl.CostEstimate(flops=24_000_000_000, bytes_accessed=22_000_000, transcendentals=0),
-    )(meta, tgt, amplitude, ladder_coupling, crossed_coupling)
-    return (driving + summed) / denominator
+    )(
+        channel_slot,
+        channel_of.reshape(1, -1),
+        source_row,
+        target_row,
+        recoupling,
+        amplitude,
+        ladder_coupling,
+        crossed_coupling,
+        driving,
+        denominator,
+    )
 
 
 def solution(mesh):

time: 113 us -> 103 us (0.912)
  other arithmetic: 7.73 us -> 0 us
  Pallas kernels: 105 us -> 101 us
  local copies, waits for them, and re-layouts: 0.19 us -> 1.91 us
    pallas_call x1, Pallas kernels: 105 us -> 101 us  [on_device(): pl.pallas_call(kernel, out_shape=jax.ShapeDtypeStruct((rows // 2, 2 * wid...]
    div x1 -> x0, other arithmetic: 2.13 us -> none  [on_device(): return (driving + summed) / denominator]
    reduce_sum x4 -> x0, other arithmetic: 2.08 us -> none  [the longest x1 0.84 us: tables(): owners = jnp.sum(jnp.where(named, channel_slot[None, :], 0), axis=1)]
    unnamed x2 -> x1, local copies, waits for them, and re-layouts: 0.01 us -> 1.91 us
    another operation x3 -> x0, other arithmetic: 1.41 us -> none  [the longest x1 0.64 us: tables(): jnp.stack([chosen.reshape(NROW, CAP), scale.reshape(NROW, CAP)], axis=1)]
    broadcast_in_dim x2 -> x0, other arithmetic: 1.35 us -> none  [place(): jnp.where(where, value[None, :] + 1, 0)]
where the time goes in v3:
time: 103 us
  Pallas kernels  101 us (98%)
  local copies, waits for them, and re-layouts  1.91 us (2%)
    pallas_call x1, Pallas kernels, on_device(): pl.pallas_call(kernel, out_shape=jax.ShapeDtypeStruct((rows // 2, 2 * wid...  101 us

profile of v3, /device:TPU:1, one launch (start us, length us, event | category | flops | bytes accessed | tf_op | source)
XLA Modules:
  0.0 102.7 jit_solution(16362256684060722993)
XLA Ops:
  0.0 100.8 %shard_map.100 = f32[50,2560]{1,0:T(8,128)} custom-call(s32[8]{0:T(128)} %channel_slot.1, s32[1,128]{1,0:T(1,128)} %bitcast.1, s32[1,128]{1,0:T(1,128)} %source_row.1, s32[1,128]{1,0:T(1,128)} %target_row.1, f32[1,128]{1,0:T(1,128)} %recoupling.1, f32[100,1280]{1,0:T(8,128)} %amp.1, f32[2560,1280]{1,0:T(8,128)} %lad.1, f32[1,1280,1280]{2,1,0:T(8,128)} %xm.1, ...), custom_call_target="tpu_custom_call" | custom-call | flops 24000000000 | bytes 22000000 | tf_op jit(solution)/shard_map/pallas_call | solution.py:427
  100.8 1.9 %copy.12 = f32[50,2560]{1,0:T(8,128)} copy(f32[50,2560]{1,0:T(8,128)} %shard_map.100) | data formatting | bytes 1024000

commit v4 on v3

--- a/solution.py
+++ b/solution.py
@@ -7,6 +7,7 @@
 
 CAP = 40
 NROW = 8
+FAR = 3
 PAD = 104
 CHUNK = 256
 MESH = pl.DeviceIdType.MESH
@@ -88,7 +89,6 @@
     load_own.wait()
     gath[r, 0:rows, :] = own[...]
     gath[r, rows:PAD, :] = jnp.zeros((PAD - rows, width), F32)
-    tables(rows, channel_slot, channel_of, source_row, target_row, recoupling, meta, tgt)
     pl.semaphore_wait(barrier, len(partners))
 
     def hop(i, shard, device, columns=None):
@@ -99,6 +99,7 @@
     g1.start()
     g2.start()
     g3.start()
+    tables(rows, channel_slot, channel_of, source_row, target_row, recoupling, meta, tgt)
     mcopies = []
     for i in range(7):
         copy = remote(meta.at[row_dev(i)], mrecv.at[r], ms.at[i], mr.at[i], (row_dev(i), c))
@@ -268,8 +269,22 @@
         ][i]
         return remote(source, zrecv.at[k, i], zs.at[k, i], zr.at[k, i], device)
 
-    def aside(k):
-        return remote(unit(k, z, 1 - yl), yrecv.at[k], ys.at[k], yr.at[k], beside)
+    quarter = CHUNK // 2
+    same, other = yl * 4, (1 - yl) * 4
+
+    def far_around(k, i):
+        source, target, device = [
+            (unit(k, zp, 1 - yl), zrecv.at[k, 0], above),
+            (unit(k, zm, 1 - yl), zrecv.at[k, 1], below),
+            (unit(k, z2, yl).at[:, 0:quarter], zrecv.at[k, 2, :, 0:quarter], above),
+            (unit(k, z2, yl).at[:, quarter:CHUNK], zrecv.at[k, 3, :, quarter:CHUNK], below),
+            (unit(k, zp, yl), zrecv.at[k, 4], above),
+            (unit(k, zm, yl), zrecv.at[k, 5], below),
+        ][i]
+        return remote(source, target, zs.at[k, i], zr.at[k, i], device)
+
+    def aside(k, i):
+        return remote(unit(k, z if i else z2, 1 - yl), yrecv.at[k, i], ys.at[k, i], yr.at[k, i], beside)
 
     def exchange(k):
         return remote(esend.at[k], erecv.at[k], es.at[k], er.at[k], sibling)
@@ -309,15 +324,46 @@
         def _():
             late(t + 1)
 
+        @pl.when((t >= FAR + 1) & (t < chunks + 1))
+        def _():
+            k = t - 1
+            aside(k, 0).wait_recv()
+            mine[k, same + z2] += yrecv[k, 0]
+            far_around(k, 2).start()
+            far_around(k, 3).start()
+
         @pl.when(t < chunks)
         def _():
             to_sibling(t).wait_recv()
             pass_on(t).wait_recv()
             scatter(t)
+
+        @pl.when(t < FAR)
+        def _():
             for i in range(4):
                 around(t, i).start()
 
-        @pl.when((t >= 1) & (t < chunks + 1))
+        @pl.when((t >= FAR) & (t < chunks))
+        def _():
+            aside(t, 0).start()
+            far_around(t, 0).start()
+            far_around(t, 1).start()
+
+        @pl.when((t >= FAR + 1) & (t < chunks + 1))
+        def _():
+            k = t - 1
+            far_around(k, 0).wait_recv()
+            far_around(k, 1).wait_recv()
+            mine[k, other + z] += zrecv[k, 0] + zrecv[k, 1]
+            aside(k, 1).start()
+            far_around(k, 2).wait_recv()
+            mine[k, same + zp, :, 0:quarter] += zrecv[k, 2, :, 0:quarter]
+            far_around(k, 4).start()
+            far_around(k, 3).wait_recv()
+            mine[k, same + zm, :, quarter:CHUNK] += zrecv[k, 3, :, quarter:CHUNK]
+            far_around(k, 5).start()
+
+        @pl.when((t >= 1) & (t < FAR + 1))
         def _():
             k = t - 1
             around(k, 0).wait_recv()
@@ -327,20 +373,27 @@
             mine[k, 4 + zm] += zrecv[k, 1]
             around(k, 5).start()
 
-        @pl.when((t >= 2) & (t < chunks + 2))
+        @pl.when((t >= 2) & (t < FAR + 2))
         def _():
             k = t - 2
             for i in range(2, 6):
                 around(k, i).wait_recv()
             mine[k, z] += zrecv[k, 3] + zrecv[k, 4]
             mine[k, 4 + z] += zrecv[k, 2] + zrecv[k, 5]
-            aside(k).start()
+            aside(k, 1).start()
 
         @pl.when((t >= 3) & (t < chunks + 3))
         def _():
             k = t - 3
-            aside(k).wait_recv()
-            mine[k, final] += yrecv[k]
+
+            @pl.when(k >= FAR)
+            def _():
+                far_around(k, 4).wait_recv()
+                far_around(k, 5).wait_recv()
+                mine[k, final] += zrecv[k, 4] + zrecv[k, 5]
+
+            aside(k, 1).wait_recv()
+            mine[k, final] += yrecv[k, 1]
             low = mine[k, final, 0:block, :]
             high = mine[k, final, block:rows, :]
             esend[k] = jnp.where(core == 0, high, low)
@@ -361,11 +414,20 @@
         for i in range(7):
             returned(k, i, row_dev(i)).wait_send()
         to_sibling(k).wait_send()
+        aside(k, 1).wait_send()
+        pass_on(k).wait_send()
+        exchange(k).wait_send()
+
+    @pl.loop(0, FAR)
+    def _(k):
         for i in range(6):
             around(k, i).wait_send()
-        aside(k).wait_send()
-        pass_on(k).wait_send()
-        exchange(k).wait_send()
+
+    @pl.loop(FAR, chunks)
+    def _(k):
+        for i in range(6):
+            far_around(k, i).wait_send()
+        aside(k, 0).wait_send()
 
 
 def tables(shard, channel_slot, channel_of, source_row, target_row, recoupling, meta, tgt):
@@ -460,7 +522,7 @@
             vmem((chunks, NROW, PAD, CHUNK), F32),
             vmem((chunks, NROW, PAD, CHUNK), F32),
             vmem((chunks, 6, PAD, CHUNK), F32),
-            vmem((chunks, PAD, CHUNK), F32),
+            vmem((chunks, 2, PAD, CHUNK), F32),
             vmem((chunks, rows // 2, CHUNK), F32),
             vmem((chunks, rows // 2, CHUNK), F32),
             vmem((rows // 2, 2 * width), F32),
@@ -479,8 +541,8 @@
             dma((chunks,)),
             dma((chunks, 6)),
             dma((chunks, 6)),
-            dma((chunks,)),
-            dma((chunks,)),
+            dma((chunks, 2)),
+            dma((chunks, 2)),
             dma((chunks,)),
             dma((chunks,)),
         ],

time: 103 us -> 98.9 us (0.960)
  Pallas kernels: 101 us -> 96.4 us
    pallas_call x1, Pallas kernels: 101 us -> 96.4 us  [on_device(): pl.pallas_call(kernel, out_shape=jax.ShapeDtypeStruct((rows // 2, 2 * wid...]
where the time goes in v4:
time: 98.9 us; the launch traced here: 98.3 us
  Pallas kernels  96.4 us (97%)
  local copies, waits for them, and re-layouts  1.91 us (2%)
    pallas_call x1, Pallas kernels, on_device(): pl.pallas_call(kernel, out_shape=jax.ShapeDtypeStruct((rows // 2, 2 * wid...  96.4 us

profile of v4, /device:TPU:1, one launch (start us, length us, event | category | flops | bytes accessed | tf_op | source)
XLA Modules:
  0.0 98.3 jit_solution(11407804098689320358)
XLA Ops:
  0.0 96.4 %shard_map.100 = f32[50,2560]{1,0:T(8,128)} custom-call(s32[8]{0:T(128)} %channel_slot.1, s32[1,128]{1,0:T(1,128)} %bitcast.1, s32[1,128]{1,0:T(1,128)} %source_row.1, s32[1,128]{1,0:T(1,128)} %target_row.1, f32[1,128]{1,0:T(1,128)} %recoupling.1, f32[100,1280]{1,0:T(8,128)} %amp.1, f32[2560,1280]{1,0:T(8,128)} %lad.1, f32[1,1280,1280]{2,1,0:T(8,128)} %xm.1, ...), custom_call_target="tpu_custom_call" | custom-call | flops 24000000000 | bytes 22000000 | tf_op jit(solution)/shard_map/pallas_call | solution.py:489
  96.4 1.9 %copy.12 = f32[50,2560]{1,0:T(8,128)} copy(f32[50,2560]{1,0:T(8,128)} %shard_map.100) | data formatting | bytes 1024000

commit v5 on v4

--- a/solution.py
+++ b/solution.py
@@ -64,8 +64,9 @@
         )
 
     def load_ladder(p):
+        first = (p // 2 + ((p + 1 + core) % 2) * chunks) * CHUNK
         return pltpu.make_async_copy(
-            lad.at[pl.ds(pl.multiple_of(p * CHUNK, CHUNK), CHUNK), :], stage.at[p % 2], stsem.at[p % 2]
+            lad.at[pl.ds(pl.multiple_of(first, CHUNK), CHUNK), :], stage.at[p % 2], stsem.at[p % 2]
         )
 
     def load_cross(p):
@@ -95,10 +96,11 @@
         ref = gath.at[shard] if columns is None else gath.at[shard, :, pl.ds(columns, half)]
         return remote(ref, ref, gs.at[i], gr.at[i], device)
 
-    g1, g2, g3 = hop(0, r, right), hop(1, r, left), hop(2, r, across)
-    g1.start()
-    g2.start()
-    g3.start()
+    n_left, n_right, n_across, n_far = xm1 * 2 + yh, xp * 2 + yh, x * 2 + 1 - yh, x2 * 2 + yh
+    sends = [hop(0, r, right, 0), hop(1, r, left, half), hop(2, r, across, 0)]
+    sends += [hop(3, r, right, half), hop(4, r, left, 0), hop(5, r, across, half)]
+    for copy in sends:
+        copy.start()
     tables(rows, channel_slot, channel_of, source_row, target_row, recoupling, meta, tgt)
     mcopies = []
     for i in range(7):
@@ -109,8 +111,7 @@
     tcopy.start()
     mrecv[r] = meta[r]
 
-    @pl.loop(0, 2 * chunks)
-    def _(p):
+    def ladder_split(p):
         load_ladder(p).wait()
 
         @pl.when(p + 1 < 2 * chunks)
@@ -120,6 +121,21 @@
         high, low = split(stage[p % 2])
         chi[p] = high
         clo[p] = low
+
+    @pl.loop(0, chunks)
+    def _(p):
+        ladder_split(p)
+
+    hop(0, n_left, right, 0).wait_recv()
+    g4 = hop(6, n_left, right, 0)
+    g4.start()
+    hop(1, n_right, left, half).wait_recv()
+    g5 = hop(7, n_right, left, half)
+    g5.start()
+
+    @pl.loop(chunks, 2 * chunks)
+    def _(p):
+        ladder_split(p)
 
     slots = NROW * CAP
     pairs = [
@@ -150,46 +166,15 @@
             else:
                 pacc[:, columns] += part
 
-    def ladder(s, k, target, h):
-        p = s * chunks + k
+    def both(k, h):
         high = ahi[2 * h : 2 * h + 2].reshape(2 * group, width)
         low = alo[2 * h : 2 * h + 2].reshape(2 * group, width)
-        value = dot_t(high, chi[p]) + dot_t(low, chi[p]) + dot_t(high, clo[p])
+        chigh = chi[pl.ds(2 * k, 2)].reshape(2 * CHUNK, width)
+        clow = clo[pl.ds(2 * k, 2)].reshape(2 * CHUNK, width)
+        value = dot_t(high, chigh) + dot_t(low, chigh) + dot_t(high, clow)
         for i in range(4):
-            target[units[4 * h + i]] = value[i * PAD : (i + 1) * PAD]
-
-    def both(k, h):
-        ladder(1 - core, k, sib.at[k], h)
-        ladder(core, k, mine.at[k], h)
-
-    n_left, n_right, n_across, n_far = xm1 * 2 + yh, xp * 2 + yh, x * 2 + 1 - yh, x2 * 2 + yh
-    hop(0, n_left, right).wait_recv()
-    g4 = hop(3, n_left, right, 0)
-    g4.start()
-    hop(1, n_right, left).wait_recv()
-    g5 = hop(4, n_right, left, half)
-    g5.start()
-    convert(1)
-    hop(2, n_across, across).wait_recv()
-    convert(0)
-
-    @pl.loop(0, 2)
-    def _(k):
-        both(k, 0)
-
-    g4.wait_send()
-    g5.wait_send()
-    g6, g7 = hop(5, n_across, right), hop(6, n_across, left)
-    g6.start()
-    g7.start()
-    hop(3, n_far, right, 0).wait_recv()
-    hop(4, n_far, left, half).wait_recv()
-    g8 = hop(7, n_far, across)
-    g8.start()
-
-    @pl.loop(2, chunks)
-    def _(k):
-        both(k, 0)
+            sib[k, units[4 * h + i]] = value[i * PAD : (i + 1) * PAD, 0:CHUNK]
+            mine[k, units[4 * h + i]] = value[i * PAD : (i + 1) * PAD, CHUNK : 2 * CHUNK]
 
     @pl.loop(0, chunks)
     def _(p):
@@ -210,20 +195,44 @@
         for row, target in ((0, colb), (1, colc)):
             column = jnp.sum(jnp.where(diagonal, mrecv[s, row : row + 1, :], 0.0), axis=1, keepdims=True)
             target[s * CAP : (s + 1) * CAP, :] = jnp.broadcast_to(column, (CAP, 128))
-    take(0)
-    take(1)
     tcopy.wait_recv()
     tall[:, 0:slots] = tgt[pl.ds(core, 1), :]
     tall[:, slots : 2 * slots] = tsib[pl.ds(core, 1), :]
     for g in range(4):
         hit = jnp.where(place(g, (group, 2 * slots), 0) == tall[...], 1.0, 0.0)
-        onehot[g] = hit.astype(BF16)
-
-    hop(5, xm1 * 2 + 1 - yh, right).wait_recv()
+        onehot[g, :, 0 : 2 * slots] = hit.astype(BF16)
+        onehot[g, :, 2 * slots : 4 * slots] = hit.astype(BF16)
+
+    hop(2, n_across, across, 0).wait_recv()
+    hop(5, n_across, across, half).wait_recv()
+    convert(0)
+    g4.wait_send()
+    g5.wait_send()
+    g6, g7 = hop(8, n_across, right), hop(9, n_across, left)
+    g6.start()
+    g7.start()
+    hop(6, n_far, right, 0).wait_recv()
+    g8 = hop(10, n_far, across, 0)
+    g8.start()
+    hop(7, n_far, left, half).wait_recv()
+    g9 = hop(11, n_far, across, half)
+    g9.start()
+    hop(3, n_left, right, half).wait_recv()
+    hop(4, n_right, left, 0).wait_recv()
+    convert(1)
+
+    @pl.loop(0, chunks)
+    def _(k):
+        both(k, 0)
+
+    take(0)
+    take(1)
+    hop(8, xm1 * 2 + 1 - yh, right).wait_recv()
     convert(2)
     take(2)
-    hop(6, xp * 2 + 1 - yh, left).wait_recv()
-    hop(7, x2 * 2 + 1 - yh, across).wait_recv()
+    hop(9, xp * 2 + 1 - yh, left).wait_recv()
+    hop(10, x2 * 2 + 1 - yh, across, 0).wait_recv()
+    hop(11, x2 * 2 + 1 - yh, across, half).wait_recv()
     convert(3)
     take(3)
     for n in range(chunks):
@@ -244,8 +253,7 @@
 
     def scatter(k):
         high, low = split(jnp.concatenate([back[k].reshape(slots, CHUNK), bsib[k].reshape(slots, CHUNK)], axis=0))
-        hits = onehot[...].reshape(4 * group, 2 * slots)
-        value = dot(hits, high) + dot(hits, low)
+        value = dot(onehot[...].reshape(4 * group, 4 * slots), jnp.concatenate([high, low], axis=0))
         for i in range(8):
             mine[k, units[i]] += value[i * PAD : (i + 1) * PAD] + crecv[k, units[i]]
 
@@ -294,9 +302,8 @@
         out[:, columns] = (drv[:, columns] + value) / den[:, columns]
 
     def late(k):
-        ladder(1 - core, k, sib.at[k], 1)
+        both(k, 1)
         to_sibling(k).start()
-        ladder(core, k, mine.at[k], 1)
 
     product(0)
     product(1)
@@ -406,7 +413,7 @@
             exchange(k).wait_recv()
             solve(k, 1 - core, erecv[k])
 
-    for copy in [g1, g2, g3, g6, g7, g8, tcopy] + mcopies:
+    for copy in sends + [g6, g7, g8, g9, tcopy] + mcopies:
         copy.wait_send()
 
     @pl.loop(0, chunks)
@@ -514,7 +521,7 @@
             vmem((slots, width), F32),
             vmem((slots, width), BF16),
             vmem((slots, width), BF16),
-            vmem((4, group, 2 * slots), BF16),
+            vmem((4, group, 4 * slots), BF16),
             vmem((chunks, NROW, CAP, CHUNK), F32),
             vmem((chunks, NROW, CAP, CHUNK), F32),
             vmem((chunks, NROW, CAP, CHUNK), F32),
@@ -529,8 +536,8 @@
             vmem((rows // 2, 2 * width), F32),
             dma((3,)),
             dma((4,)),
-            dma((8,)),
-            dma((8,)),
+            dma((12,)),
+            dma((12,)),
             dma((8,)),
             dma((8,)),
             dma((chunks, 7)),

time: 98.9 us -> 95.9 us (0.970)
  Pallas kernels: 96.4 us -> 93.5 us
    pallas_call x1, Pallas kernels: 96.4 us -> 93.5 us  [on_device(): pl.pallas_call(kernel, out_shape=jax.ShapeDtypeStruct((rows // 2, 2 * wid...]
where the time goes in v5:
time: 95.9 us; the launch traced here: 95.4 us
  Pallas kernels  93.5 us (97%)
  local copies, waits for them, and re-layouts  1.91 us (2%)
    pallas_call x1, Pallas kernels, on_device(): pl.pallas_call(kernel, out_shape=jax.ShapeDtypeStruct((rows // 2, 2 * wid...  93.5 us

profile of v5, /device:TPU:1, one launch (start us, length us, event | category | flops | bytes accessed | tf_op | source)
XLA Modules:
  0.0 95.4 jit_solution(1430048391242793457)
XLA Ops:
  0.0 93.5 %shard_map.100 = f32[50,2560]{1,0:T(8,128)} custom-call(s32[8]{0:T(128)} %channel_slot.1, s32[1,128]{1,0:T(1,128)} %bitcast.1, s32[1,128]{1,0:T(1,128)} %source_row.1, s32[1,128]{1,0:T(1,128)} %target_row.1, f32[1,128]{1,0:T(1,128)} %recoupling.1, f32[100,1280]{1,0:T(8,128)} %amp.1, f32[2560,1280]{1,0:T(8,128)} %lad.1, f32[1,1280,1280]{2,1,0:T(8,128)} %xm.1, ...), custom_call_target="tpu_custom_call" | custom-call | flops 24000000000 | bytes 22000000 | tf_op jit(solution)/shard_map/pallas_call | solution.py:496
  93.5 1.9 %copy.12 = f32[50,2560]{1,0:T(8,128)} copy(f32[50,2560]{1,0:T(8,128)} %shard_map.100) | data formatting | bytes 1024000

commit v6 on v5

--- a/solution.py
+++ b/solution.py
@@ -245,7 +245,8 @@
         return remote(cross.at[k, source], back.at[k, r], ts.at[k, i], tr.at[k, i], (source, c))
 
     def product(k):
-        value = dot(phi[...], xhi[k]) + dot(plo[...], xhi[k]) + dot(phi[...], xlo[k])
+        twice = dot(jnp.concatenate([phi[...], plo[...]], axis=0), xhi[k])
+        value = twice[0:slots] + twice[slots : 2 * slots] + dot(phi[...], xlo[k])
         cross[k] = value.reshape(NROW, CAP, CHUNK)
         for i in range(7):
             returned(k, i, row_dev(i)).start()

time: 95.9 us -> 95.7 us (level)
  no operation moved by 1% of the time
where the time goes in v6:
time: 95.7 us; the launch traced here: 95.1 us
  Pallas kernels  93.2 us (97%)
  local copies, waits for them, and re-layouts  1.91 us (2%)
    pallas_call x1, Pallas kernels, on_device(): pl.pallas_call(kernel, out_shape=jax.ShapeDtypeStruct((rows // 2, 2 * wid...  93.2 us

profile of v6, /device:TPU:1, one launch (start us, length us, event | category | flops | bytes accessed | tf_op | source)
XLA Modules:
  0.0 95.1 jit_solution(8255395792439644964)
XLA Ops:
  0.0 93.2 %shard_map.100 = f32[50,2560]{1,0:T(8,128)} custom-call(s32[8]{0:T(128)} %channel_slot.1, s32[1,128]{1,0:T(1,128)} %bitcast.1, s32[1,128]{1,0:T(1,128)} %source_row.1, s32[1,128]{1,0:T(1,128)} %target_row.1, f32[1,128]{1,0:T(1,128)} %recoupling.1, f32[100,1280]{1,0:T(8,128)} %amp.1, f32[2560,1280]{1,0:T(8,128)} %lad.1, f32[1,1280,1280]{2,1,0:T(8,128)} %xm.1, ...), custom_call_target="tpu_custom_call" | custom-call | flops 24000000000 | bytes 22000000 | tf_op jit(solution)/shard_map/pallas_call | solution.py:497
  93.2 1.9 %copy.12 = f32[50,2560]{1,0:T(8,128)} copy(f32[50,2560]{1,0:T(8,128)} %shard_map.100) | data formatting | bytes 1024000
